TPU v7x, 32 devices: a whole 2x2x4 slice. The times are simulated.
32 devices in a mesh: expert: 16 (over z, y, x), tensor: 2 (over core).
Axes of the slice: x: 2, y: 2, z: 4, core: 2. Of those that a mesh axis runs over, the one named last changes fastest.
Arguments:
- hidden_in: bfloat16 [16384, 768], P('expert'), may hold values from -6 to 6
- w_qkv: bfloat16 [768, 3, 768], P(None, None, 'tensor'), may hold values from -0.21875 to 0.21875
- w_out: bfloat16 [768, 768], P('tensor'), may hold values from -0.875 to 0.875
- gain_in: float32 [768], replicated, may hold values from 0.5 to 1.5
- gain_mid: float32 [768], replicated, may hold values from 0.5 to 1.5
- w_router: bfloat16 [768, 12], replicated, may hold values from -0.109375 to 0.109375
- w_const: bfloat16 [768, 4], replicated, may hold values from -0.21875 to 0.21875
- const_vec: float32 [2, 768], replicated, may hold values from -5 to 5
- w_gate: bfloat16 [8, 768, 2048], P(None, 'expert', 'tensor'), may hold values from -0.21875 to 0.21875
- w_up: bfloat16 [8, 768, 2048], P(None, 'expert', 'tensor'), may hold values from -0.21875 to 0.21875
- w_down: bfloat16 [8, 768, 2048], P(None, 'expert', 'tensor'), may hold values from -0.125 to 0.125
- prev_logits: float32 [16384, 12], P('expert'), may hold values from -3 to 3
- routes: int32 [16384, 2], P('expert'), may hold values from 0 to 11, all different within a row
- doc_ids: int32 [16384], P('expert'), may hold values from 0 to 3, as said below
- span_start: int32 [16, 2], P('expert'), may hold values from 0 to 768, as said below
- span_len: int32 [16, 2], P('expert'), may hold values from 64 to 256, as said below
- d_output: bfloat16 [16384, 768], P('expert'), may hold values from -6 to 6
Outputs:
- output: bfloat16 [16384, 768], P('expert')
- grad_input: bfloat16 [16384, 768], P('expert')
- grad_prev: float32 [16384, 12], P('expert')
- grad_qkv: float32 [768, 3, 768], P('expert', None, 'tensor')
- grad_wout: float32 [768, 768], P('tensor', 'expert')
- grad_gain_in: float32 [768], P('expert')
- grad_gain_mid: float32 [768], P('expert')
- grad_router: float32 [768, 12], P('expert')
- grad_const: float32 [768, 4], P('expert')
- grad_cvec: float32 [2, 768], P(None, 'expert')
- grad_gate: float32 [8, 768, 2048], P(None, 'expert', 'tensor')
- grad_up: float32 [8, 768, 2048], P(None, 'expert', 'tensor')
- grad_down: float32 [8, 768, 2048], P(None, 'expert', 'tensor')
Inputs may be any that keep to these rules, and one draw needn't show every extreme that they name: routes below 8 name feed-forward experts; 8 is the zero expert, 9 the copy expert, 10 and 11 the constant experts. `doc_ids`: within each sequence ids never fall and split it into up to four documents; some sequence is a single document. `span_start`: span j of a sequence lies inside the j-th of 2 equal parts of it. `span_len`: some span of every sequence has exactly 256 tokens.
All inputs are finite; a program needn't handle non-finite values.
Results may differ from a plain program's by a relative error of at most 0.017.
Values may be sent and summed in bfloat16 or wider, within the bound.
No kernel may reach another device: no remote copies, remote signals or barrier semaphores. Data moves between devices by JAX's collectives and lax.ppermute only.
A program may use at most 192 MiB of HBM per device.

v0:
```python
import jax
import jax.numpy as jnp
from jax import lax
from jax.sharding import PartitionSpec as P

HD = 64
CAP = 176


EPSILON = 1e-06


def norm_forward(values, gain_vec):
    inverse = lax.rsqrt(jnp.mean(values * values, axis=-1, keepdims=True) + EPSILON)
    return (values * inverse * gain_vec, inverse)


def norm_backward(values, inverse, gain_vec, upstream):
    gain_grad = jnp.sum(upstream * values * inverse, axis=0)
    scaled = upstream * gain_vec
    value_grad = inverse * scaled - values * inverse**3 * jnp.mean(
        scaled * values, axis=-1, keepdims=True
    )
    return (gain_grad, value_grad)


def angles(length):
    half_dim = HD // 2
    position = jnp.arange(length).astype(jnp.float32)
    frequency = 10000.0 ** (-jnp.arange(half_dim).astype(jnp.float32) / half_dim)
    phase_tab = position[:, None] * frequency[None, :]
    return (jnp.cos(phase_tab)[:, None, :], jnp.sin(phase_tab)[:, None, :])


def rotate(values, cosine, sine_tab):
    half_dim = values.shape[-1] // 2
    first_half = values[..., :half_dim]
    second_half = values[..., half_dim:]
    return jnp.concatenate(
        [
            first_half * cosine - second_half * sine_tab,
            second_half * cosine + first_half * sine_tab,
        ],
        axis=-1,
    )


def rotate_back(values, cosine, sine_tab):
    half_dim = values.shape[-1] // 2
    first_half = values[..., :half_dim]
    second_half = values[..., half_dim:]
    return jnp.concatenate(
        [
            first_half * cosine + second_half * sine_tab,
            second_half * cosine - first_half * sine_tab,
        ],
        axis=-1,
    )


def span_index(starts, lengths, length):
    position = jnp.arange(length)[:, None]
    inside = (position >= starts[None, :]) & (position < starts[None, :] + lengths[None, :])
    return jnp.sum(jnp.where(inside, jnp.arange(1, starts.shape[0] + 1)[None, :], 0), axis=1)


def local(
    hidden_in,
    w_qkv,
    w_out,
    gain_in,
    gain_mid,
    w_router,
    w_const,
    const_vec,
    w_gate,
    w_up,
    w_down,
    prev_logits,
    routes,
    doc_ids,
    span_start,
    span_len,
    d_output,
):
    length, model_width = hidden_in.shape
    local_heads = w_qkv.shape[2] // HD
    route_count = w_router.shape[1]
    expert_total = route_count - 4
    peer_count = lax.axis_size("expert")
    copies = peer_count // expert_total
    capacity = CAP
    block_len = min(512, length)
    block_count = length // block_len
    score_scale = HD ** (-0.5)
    head_shape = (length, local_heads, HD)
    row_share = w_gate.shape[1]
    unit_share = w_gate.shape[2]
    fetched = (
        lax.all_to_all(
            jnp.repeat(w_gate, copies, axis=0), "expert", split_axis=0, concat_axis=1, tiled=True
        ),
        lax.all_to_all(
            jnp.repeat(w_up, copies, axis=0), "expert", split_axis=0, concat_axis=1, tiled=True
        ),
        lax.all_to_all(
            jnp.repeat(w_down, copies, axis=0), "expert", split_axis=0, concat_axis=1, tiled=True
        ),
    )
    own_gate = fetched[0][0]
    own_up = fetched[1][0]
    own_down = fetched[2][0]
    hidden_f = hidden_in.astype(jnp.float32)
    normed_in_f, inverse_in = norm_forward(hidden_f, gain_in)
    normed_in = normed_in_f.astype(jnp.bfloat16)
    projected = jnp.einsum("td,dce->tce", normed_in, w_qkv, preferred_element_type=jnp.float32)
    cosine, sine_tab = angles(length)
    queries = rotate(projected[:, 0].reshape(head_shape), cosine, sine_tab).astype(jnp.bfloat16)
    keys_rot = rotate(projected[:, 1].reshape(head_shape), cosine, sine_tab).astype(jnp.bfloat16)
    value_rows = projected[:, 2].reshape(head_shape).astype(jnp.bfloat16)
    positions = jnp.arange(length)
    span_of = span_index(span_start[0], span_len[0], length)

    def block_scores(row_start):
        query_blk = lax.dynamic_slice_in_dim(queries, row_start, block_len, 0)
        query_pos = row_start + jnp.arange(block_len)
        doc_blk = lax.dynamic_slice_in_dim(doc_ids, row_start, block_len, 0)
        span_blk = lax.dynamic_slice_in_dim(span_of, row_start, block_len, 0)
        same_span = (span_blk[:, None] == span_of[None, :]) & (span_blk[:, None] > 0)
        visible = (doc_blk[:, None] == doc_ids[None, :]) & (
            (positions[None, :] <= query_pos[:, None]) | same_span
        )
        raw_scores = (
            jnp.einsum("qhe,khe->hqk", query_blk, keys_rot, preferred_element_type=jnp.float32)
            * score_scale
        )
        return (jnp.where(visible[None], raw_scores, -1e30), query_blk)

    def forward_block(block_idx):
        scores, unused = block_scores(block_idx * block_len)
        row_max = jnp.max(scores, axis=-1, keepdims=True)
        log_total = row_max + jnp.log(jnp.sum(jnp.exp(scores - row_max), axis=-1, keepdims=True))
        soft_probs = jnp.exp(scores - log_total)
        context = jnp.einsum(
            "hqk,khe->qhe",
            soft_probs.astype(jnp.bfloat16),
            value_rows,
            preferred_element_type=jnp.float32,
        )
        return (context, log_total)

    contexts, log_totals = lax.map(forward_block, jnp.arange(block_count))
    context_b = contexts.reshape(length, local_heads * HD).astype(jnp.bfloat16)
    attended = lax.psum(jnp.dot(context_b, w_out, preferred_element_type=jnp.float32), "tensor")
    residual_mid = hidden_f + attended
    normed_mid_f, inverse_mid = norm_forward(residual_mid, gain_mid)
    normed_mid = normed_mid_f.astype(jnp.bfloat16)
    joint_weight = jnp.concatenate([w_router, w_const], axis=1)
    route_mix = jnp.dot(normed_mid, joint_weight, preferred_element_type=jnp.float32)
    logits = route_mix[:, :route_count] + prev_logits
    const_logits = route_mix[:, route_count:]
    route_hot = routes[:, :, None] == jnp.arange(route_count)[None, None, :]
    chosen = jnp.sum(jnp.where(route_hot, logits[:, None, :], 0.0), axis=-1)
    gate_probs = jax.nn.softmax(chosen, axis=1)
    flat_routes = routes.reshape(2 * length)
    flat_hot = route_hot.reshape(2 * length, route_count).astype(jnp.int32)
    earlier = jnp.cumsum(flat_hot, axis=0) - flat_hot
    slot_pos = jnp.sum(earlier * flat_hot, axis=1)
    kept_pair = (flat_routes < expert_total) & (slot_pos < capacity)
    slot_of = jnp.where(kept_pair, flat_routes * capacity + slot_pos, expert_total * capacity)
    slot_pair = (
        jnp.full((expert_total * capacity + 1,), 2 * length, jnp.int32)
        .at[slot_of]
        .set(jnp.arange(2 * length, dtype=jnp.int32))[:-1]
    )
    zero_row = jnp.zeros((1, model_width), jnp.bfloat16)
    padded_in = jnp.concatenate([normed_mid, zero_row], axis=0)
    send_rows = padded_in[slot_pair // 2].reshape(peer_count, capacity // copies, model_width)
    recv_rows = lax.all_to_all(send_rows, "expert", split_axis=0, concat_axis=0, tiled=True)
    gate_pre = jnp.einsum("scd,df->scf", recv_rows, own_gate, preferred_element_type=jnp.float32)
    up_pre = jnp.einsum("scd,df->scf", recv_rows, own_up, preferred_element_type=jnp.float32)
    hidden = (jax.nn.silu(gate_pre) * up_pre).astype(jnp.bfloat16)
    partial_value = jnp.einsum("scf,df->scd", hidden, own_down, preferred_element_type=jnp.float32)
    summed = lax.psum(partial_value.astype(jnp.bfloat16), "tensor")
    returned = lax.all_to_all(summed, "expert", split_axis=0, concat_axis=0, tiled=True)
    exchanged = returned
    returned = exchanged
    padded_out = jnp.concatenate(
        [returned.reshape(expert_total * capacity, model_width), zero_row], axis=0
    )
    pair_out = padded_out[slot_of].reshape(length, 2, model_width).astype(jnp.float32)
    mixing = jax.nn.softmax(const_logits.reshape(length, 2, 2), axis=-1)
    const_out = (
        mixing[:, :, 0:1] * normed_mid_f[:, None, :] + mixing[:, :, 1:2] * const_vec[None, :, :]
    )
    route_col = routes[:, :, None]
    pair_out = pair_out + jnp.where(route_col == expert_total + 1, normed_mid_f[:, None, :], 0.0)
    pair_out = pair_out + jnp.where(route_col == expert_total + 2, const_out[:, 0:1, :], 0.0)
    pair_out = pair_out + jnp.where(route_col == expert_total + 3, const_out[:, 1:2, :], 0.0)
    output = (residual_mid + jnp.sum(gate_probs[:, :, None] * pair_out, axis=1)).astype(
        jnp.bfloat16
    )
    out_grad = d_output.astype(jnp.float32)
    gate_grad = jnp.sum(out_grad[:, None, :] * pair_out, axis=-1)
    chosen_grad = gate_probs * (gate_grad - jnp.sum(gate_probs * gate_grad, axis=1, keepdims=True))
    prev_grad = jnp.sum(jnp.where(route_hot, chosen_grad[:, :, None], 0.0), axis=1)
    const_hot = route_col == expert_total + 2 + jnp.arange(2)[None, None, :]
    const_weight = jnp.sum(jnp.where(const_hot, gate_probs[:, :, None], 0.0), axis=1)
    const_grad = const_weight[:, :, None] * out_grad[:, None, :]
    mixing_grad = jnp.stack(
        [
            jnp.sum(const_grad * normed_mid_f[:, None, :], axis=-1),
            jnp.sum(const_grad * const_vec[None, :, :], axis=-1),
        ],
        axis=-1,
    )
    logit_grad = mixing * (mixing_grad - jnp.sum(mixing * mixing_grad, axis=-1, keepdims=True))
    grad_cvec = jnp.sum(mixing[:, :, 1:2] * const_grad, axis=0)
    joint_grad = jnp.concatenate([prev_grad, logit_grad.reshape(length, 4)], axis=1).astype(
        jnp.bfloat16
    )
    copy_weight = jnp.sum(jnp.where(routes == expert_total + 1, gate_probs, 0.0), axis=1)
    direct_grad = copy_weight[:, None] * out_grad + jnp.sum(mixing[:, :, 0:1] * const_grad, axis=1)
    pair_grad = (
        (gate_probs[:, :, None] * out_grad[:, None, :])
        .astype(jnp.bfloat16)
        .reshape(2 * length, model_width)
    )
    slot_grad = jnp.concatenate([pair_grad, zero_row], axis=0)[slot_pair].reshape(
        peer_count, capacity // copies, model_width
    )
    recv_grad, recv_rows = (
        lax.all_to_all(slot_grad, "expert", split_axis=0, concat_axis=0, tiled=True),
        lax.all_to_all(send_rows, "expert", split_axis=0, concat_axis=0, tiled=True),
    )
    gate_pre = jnp.einsum("scd,df->scf", recv_rows, own_gate, preferred_element_type=jnp.float32)
    up_pre = jnp.einsum("scd,df->scf", recv_rows, own_up, preferred_element_type=jnp.float32)
    sigmoid_g = jax.nn.sigmoid(gate_pre)
    activated = gate_pre * sigmoid_g
    hidden = (activated * up_pre).astype(jnp.bfloat16)
    hidden_grad = jnp.einsum("scd,df->scf", recv_grad, own_down, preferred_element_type=jnp.float32)
    own_down_grad = jnp.einsum("scd,scf->df", recv_grad, hidden, preferred_element_type=jnp.float32)
    gate_pre_grad = (
        hidden_grad * up_pre * sigmoid_g * (1.0 + gate_pre * (1.0 - sigmoid_g))
    ).astype(jnp.bfloat16)
    up_pre_grad = (hidden_grad * activated).astype(jnp.bfloat16)
    own_gate_grad = jnp.einsum(
        "scd,scf->df", recv_rows, gate_pre_grad, preferred_element_type=jnp.float32
    )
    own_up_grad = jnp.einsum(
        "scd,scf->df", recv_rows, up_pre_grad, preferred_element_type=jnp.float32
    )
    row_grad = jnp.einsum(
        "scf,df->scd", gate_pre_grad, own_gate, preferred_element_type=jnp.float32
    )
    row_grad = row_grad + jnp.einsum(
        "scf,df->scd", up_pre_grad, own_up, preferred_element_type=jnp.float32
    )
    row_grad = lax.psum(row_grad.astype(jnp.bfloat16), "tensor")
    row_back = lax.all_to_all(row_grad, "expert", split_axis=0, concat_axis=0, tiled=True)
    from_slots = jnp.concatenate(
        [row_back.reshape(expert_total * capacity, model_width), zero_row], axis=0
    )[slot_of]
    from_slots = jnp.sum(from_slots.reshape(length, 2, model_width).astype(jnp.float32), axis=1)
    mid_grad = (
        from_slots
        + jnp.einsum("tr,dr->td", joint_grad, joint_weight, preferred_element_type=jnp.float32)
        + direct_grad
    )
    joint_weight_grad = jnp.einsum(
        "td,tr->dr", normed_mid, joint_grad, preferred_element_type=jnp.float32
    )
    grad_gain_mid, residual_grad = norm_backward(residual_mid, inverse_mid, gain_mid, mid_grad)
    residual_grad = residual_grad + out_grad
    parted = (
        lax.all_to_all(
            own_gate_grad[None].astype(jnp.bfloat16),
            "expert",
            split_axis=1,
            concat_axis=0,
            tiled=True,
        ).astype(jnp.float32),
        lax.all_to_all(
            own_up_grad[None].astype(jnp.bfloat16),
            "expert",
            split_axis=1,
            concat_axis=0,
            tiled=True,
        ).astype(jnp.float32),
        lax.all_to_all(
            own_down_grad[None].astype(jnp.bfloat16),
            "expert",
            split_axis=1,
            concat_axis=0,
            tiled=True,
        ).astype(jnp.float32),
    )
    grad_gate = jnp.sum(parted[0].reshape(expert_total, copies, row_share, unit_share), axis=1)
    grad_up = jnp.sum(parted[1].reshape(expert_total, copies, row_share, unit_share), axis=1)
    grad_down = jnp.sum(parted[2].reshape(expert_total, copies, row_share, unit_share), axis=1)
    attended_grad = residual_grad.astype(jnp.bfloat16)
    grad_wout = jnp.einsum(
        "te,td->ed", context_b, attended_grad, preferred_element_type=jnp.float32
    )
    context_grad = (
        jnp.einsum("td,ed->te", attended_grad, w_out, preferred_element_type=jnp.float32)
        .astype(jnp.bfloat16)
        .reshape(head_shape)
    )

    def backward_block(totals, block_idx):
        key_grad, value_grad = totals
        row_start = block_idx * block_len
        scores, query_blk = block_scores(row_start)
        soft_probs = jnp.exp(scores - log_totals[block_idx])
        grad_blk = lax.dynamic_slice_in_dim(context_grad, row_start, block_len, 0)
        value_grad = value_grad + jnp.einsum(
            "hqk,qhe->khe",
            soft_probs.astype(jnp.bfloat16),
            grad_blk,
            preferred_element_type=jnp.float32,
        )
        prob_grad = jnp.einsum(
            "qhe,khe->hqk", grad_blk, value_rows, preferred_element_type=jnp.float32
        )
        score_grad = (
            soft_probs * (prob_grad - jnp.sum(soft_probs * prob_grad, axis=-1, keepdims=True))
        ).astype(jnp.bfloat16)
        query_grad = score_scale * jnp.einsum(
            "hqk,khe->qhe", score_grad, keys_rot, preferred_element_type=jnp.float32
        )
        key_grad = key_grad + score_scale * jnp.einsum(
            "hqk,qhe->khe", score_grad, query_blk, preferred_element_type=jnp.float32
        )
        return ((key_grad, value_grad), query_grad)

    zeros_heads = jnp.zeros(head_shape, jnp.float32)
    (key_grad, value_grad), query_grads = lax.scan(
        backward_block, (zeros_heads, zeros_heads), jnp.arange(block_count)
    )
    query_grad = rotate_back(query_grads.reshape(head_shape), cosine, sine_tab)
    key_grad = rotate_back(key_grad, cosine, sine_tab)
    projected_grad = jnp.stack(
        [
            query_grad.reshape(length, local_heads * HD),
            key_grad.reshape(length, local_heads * HD),
            value_grad.reshape(length, local_heads * HD),
        ],
        axis=1,
    ).astype(jnp.bfloat16)
    grad_qkv = jnp.einsum(
        "td,tce->dce", normed_in, projected_grad, preferred_element_type=jnp.float32
    )
    normed_grad = lax.psum(
        jnp.einsum("tce,dce->td", projected_grad, w_qkv, preferred_element_type=jnp.float32).astype(
            jnp.bfloat16
        ),
        "tensor",
    ).astype(jnp.float32)
    grad_gain_in, input_grad = norm_backward(hidden_f, inverse_in, gain_in, normed_grad)
    grad_input = (residual_grad + input_grad).astype(jnp.bfloat16)
    reduced = (
        lax.psum_scatter(grad_qkv, "expert", scatter_dimension=0, tiled=True),
        lax.psum_scatter(grad_wout, "expert", scatter_dimension=1, tiled=True),
        lax.psum_scatter(grad_gain_in, "expert", scatter_dimension=0, tiled=True),
        lax.psum_scatter(grad_gain_mid, "expert", scatter_dimension=0, tiled=True),
        lax.psum_scatter(
            joint_weight_grad[:, :route_count], "expert", scatter_dimension=0, tiled=True
        ),
        lax.psum_scatter(
            joint_weight_grad[:, route_count:], "expert", scatter_dimension=0, tiled=True
        ),
        lax.psum_scatter(grad_cvec, "expert", scatter_dimension=1, tiled=True),
    )
    return (
        output,
        grad_input,
        prev_grad,
        reduced[0],
        reduced[1],
        reduced[2],
        reduced[3],
        reduced[4],
        reduced[5],
        reduced[6],
        grad_gate,
        grad_up,
        grad_down,
    )


def solution(mesh):
    placed = (
        P("expert", None),
        P(None, None, "tensor"),
        P("tensor", None),
        P(),
        P(),
        P(),
        P(),
        P(),
        P(None, "expert", "tensor"),
        P(None, "expert", "tensor"),
        P(None, "expert", "tensor"),
        P("expert", None),
        P("expert", None),
        P("expert"),
        P("expert", None),
        P("expert", None),
        P("expert", None),
    )
    return jax.shard_map(
        local,
        mesh=mesh,
        in_specs=placed,
        out_specs=(
            P("expert", None),
            P("expert", None),
            P("expert", None),
            P("expert", None, "tensor"),
            P("tensor", "expert"),
            P("expert"),
            P("expert"),
            P("expert", None),
            P("expert", None),
            P(None, "expert"),
            P(None, "expert", "tensor"),
            P(None, "expert", "tensor"),
            P(None, "expert", "tensor"),
        ),
        check_vma=False,
    )
```

profile of v0, /device:TPU:0, one launch (start us, length us, event | category | flops | bytes accessed | tf_op | source)
XLA Modules:
  0.0 1318.9 jit_solution(7564542240118713534)
XLA Ops:
  9.8 8.4 all-to-all-start.1
  28.3 24.2 %all-to-all-done.1 = bf16[16,48,1024]{2,1,0:T(8,128)(2,1)} async-done(((bf16[16,48,1024]{2,1,0:T(8,128)(2,1)}), bf16[16,48,1024]{2,1,0:T(8,128)(2,1)}, u32[]{:S(2)}, u32[]{:S(2)}) %all-to-all-start.1) | async-done | bytes 1572896 | tf_op jit(solution)/shard_map/all_to_all | solution.py:100
  54.9 7.7 all-to-all-start.2
  63.0 36.7 %while.28 = (s32[]{:T(128)}, bf16[2,512,6,64]{1,3,2,0:T(8,128)(2,1)}, f32[2,6,512,1]{2,1,3,0:T(8,128)S(1)}, s32[2]{0:T(128)S(1)}, s32[1024]{0:T(1024)S(1)}, /*in...) while((s32[]{:T(128)}, ...), condition=%wide.region_5.6_spmd.clone, body=%wide.region_2.5_spmd.clone.sunk | while | flops 843053056 | bytes 102511928 | solution.py:152
  72.6 7.8 fusion.150
  91.0 7.8 fusion.150
  108.4 7.6 all-to-all-start.3
  116.7 6.1 reduce-window.6
  128.8 8.0 scatter_custom_fusion
  143.3 5.6 gather_fusion
  148.9 7.3 all-to-all-start
  160.6 8.6 mul.590
  176.2 8.9 gather_fusion.2
  185.1 14.8 %all-to-all-done = bf16[16,88,768]{2,1,0:T(8,128)(2,1)} async-done(((bf16[16,88,768]{2,1,0:T(8,128)(2,1)}), bf16[16,88,768]{2,1,0:T(8,128)(2,1)}, u32[]{:S(2)}, u32[]{:S(2)}) %all-to-all-start) | async-done | bytes 2162720 | tf_op jit(solution)/shard_map/all_to_all | solution.py:179
  199.9 9.9 all-to-all-start.5
  210.0 6.9 fusion.93
  217.0 6.9 fusion.94
  223.9 29.2 %all-to-all-done.5 = bf16[16,88,768]{2,1,0:T(8,128)(2,1)} async-done(((bf16[16,88,768]{2,1,0:T(8,128)(2,1)}), bf16[16,88,768]{2,1,0:T(8,128)(2,1)}, u32[]{:S(2)}, u32[]{:S(2)}) %all-to-all-start.5) | async-done | bytes 2162720 | tf_op jit(solution)/shard_map/all_to_all | solution.py:233
  253.1 8.8 multiply_convert_fusion.2
  267.1 5.3 convolution_convert_fusion
  272.4 5.4 add_convert_fusion
  277.8 33.3 %all-reduce.16.cloned.1.call-done = (bf16[16,88,768]{2,1,0:T(8,128)(2,1)}, bf16[16,88,768]{2,1,0:T(8,128)(2,1)}) async-done(((bf16[16,88,768]{2,1,0:T(8,128)(2,1)}, bf16[16,88,768]{2,1,0:T(8,128)(2,1)}), (bf16[16,88,768]{2,1,0:T(8,128)(2,1)}, bf16[16,88,768]{2,1,0:T(8,128)(2,1)})) %all-reduce.16.cloned.1.call-update) | async-done | bytes 4325392 | tf_op jit(solution)/shard_map/psum | solution.py:184
  311.0 7.1 all-to-all-start.4
  328.7 8.0 multiply_add_fusion
  336.7 13.0 fusion.89
  362.4 10.9 all-to-all-start.6
  376.5 12.4 gather_fusion.1
  388.9 7.8 reshape.683
  396.7 47.2 %fusion.41 = (f32[2,768]{1,0:T(2,128)}, f32[1024,768]{1,0:T(8,128)}, f32[1024,2]{1,0:T(8,128)}, f32[1024,2]{1,0:T(8,128)}, f32[1024,768]{1,0:T(8,128)}, /*index=5*/f32[1024,2]{1,0:T(8,128)}) fusion(f32[1024,2]{1,0:T(8,128)} %copy.136, f32[1024,768]{1,0:T(8,128)} %convert_element_type.236, f32[1024,2]{1,0:T(8,128)} %bitcast.219, f32[1024,2]{1,0:T(8,128)} %bitcast.217, ...), kind=kLoop, calls=%fused_computation.69 | loop fusion | flops 28303872 | bytes 25241600 | tf_op jit(solution)/shard_map/reduce_sum | solution.py:218
  452.4 12.0 gather_fusion.3
  464.4 8.0 reshape.684
  472.4 11.9 reduce_sum.263
  485.2 5.6 multiply_reduce_fusion.3
  496.2 129.4 %while.29 = (s32[]{:T(128)}, f32[1024,6,64]{0,2,1:T(8,128)}, f32[1024,6,64]{0,2,1:T(8,128)}, f32[2,512,6,64]{1,0,3,2:T(2,128)}, s32[2]{0:T(128)S(1)}, /*index=5*...) while((s32[]{:T(128)}, f32[1024,6,64]{0,2,1:T(8,128)}, ...), condition=%wide.region_33.34_spmd.clone, body=%wide.region_31.33_spmd.clone.sunk | while | flops 2065758208 | bytes 176801168 | solution.py:338
  499.1 7.4 fusion.160
  508.5 11.6 multiply_reduce_fusion.9
  521.5 6.9 multiply_convert_fusion.7
  532.7 15.0 %dynamic_update_slice.21 = f32[2,512,6,64]{1,0,3,2:T(2,128)} dynamic-update-slice(f32[2,512,6,64]{1,0,3,2:T(2,128)} %get-tuple-element.522, f32[1,512,6,64]{1,0,3,2:T(1,128)} %copy.202, s32[]{:T(128)} %get-tuple-element.519, s32[]{:T(128)} %constant.57.clone.1..sunk.1, s32[]{:T(128)} %constant.57.clone.1..sunk.1, s32[]{:T(128)} %constant.57.clone.1..sunk.1) | dynamic-update-slice | bytes 1572868 | tf_op jit(solution)/shard_map/while/body/jit(dynamic_update_index_in_dim)/dynamic_update_slice | solution.py:152
  547.8 5.3 bitcast_add_fusion.4
  553.1 7.6 bitcast_add_fusion.5
  563.2 7.4 fusion.160
  572.6 11.6 multiply_reduce_fusion.9
  585.6 6.9 multiply_convert_fusion.7
  596.8 15.0 %dynamic_update_slice.21 = f32[2,512,6,64]{1,0,3,2:T(2,128)} dynamic-update-slice(f32[2,512,6,64]{1,0,3,2:T(2,128)} %get-tuple-element.522, f32[1,512,6,64]{1,0,3,2:T(1,128)} %copy.202, s32[]{:T(128)} %get-tuple-element.519, s32[]{:T(128)} %constant.57.clone.1..sunk.1, s32[]{:T(128)} %constant.57.clone.1..sunk.1, s32[]{:T(128)} %constant.57.clone.1..sunk.1) | dynamic-update-slice | bytes 1572868 | tf_op jit(solution)/shard_map/while/body/jit(dynamic_update_index_in_dim)/dynamic_update_slice | solution.py:152
  611.8 5.8 bitcast_add_fusion.4
  617.6 8.1 bitcast_add_fusion.5
  650.2 5.1 fusion.57
  659.9 12.8 reduce.8
  677.8 6.9 all-to-all-start.9
  684.8 5.8 fusion.59
  699.9 12.5 reduce.6
  718.0 7.3 all-to-all-start.7
  734.5 12.6 reduce.7
  752.1 8.0 all-to-all-done.7
  760.1 7.3 all-to-all-start.8
  768.7 10.0 reshape.755
  786.5 10.0 reshape.751
  804.4 10.0 reshape.753
  823.7 72.0 %reduce-scatter.18.cloned.1.call-done = f32[48,4]{1,0:T(8,128)} async-done(((f32[768,4]{1,0:T(8,128)}), f32[48,4]{1,0:T(8,128)}) %reduce-scatter.18.cloned.1.call-update) | async-done | bytes 784
  897.1 123.8 %reduce-scatter.16.cloned.1.call-done = f32[48,12]{1,0:T(8,128)} async-done(((f32[768,12]{1,0:T(8,128)}), f32[48,12]{1,0:T(8,128)}) %reduce-scatter.16.cloned.1.call-update) | async-done | bytes 2320
  1022.3 21.0 %all-reduce.14.cloned.1.call-done = bf16[1024,768]{1,0:T(8,128)(2,1)} async-done(((bf16[1024,768]{1,0:T(8,128)(2,1)}), bf16[1024,768]{1,0:T(8,128)(2,1)}) %all-reduce.14.cloned.1.call-update) | async-done | bytes 1572880 | tf_op jit(solution)/shard_map/psum | solution.py:354
  1046.1 42.7 %all-reduce.6 = (f32[768]{0:T(1024)S(1)}, f32[768]{0:T(1024)S(1)}) all-reduce(f32[768]{0:T(1024)S(1)} %get-tuple-element.211, f32[768]{0:T(1024)S(1)} %copy-done.73), channel_id=4, replica_groups=mesh['expert'=16,'tensor'=2] {'expert'}, use_global_device_ids=true, to_apply=%region_39.40.clone | all-reduce | flops 1536 | bytes 12288
  1093.7 79.7 %reduce-scatter.14.cloned.1.call-done = f32[384,48]{0,1:T(8,128)} async-done(((f32[384,768]{0,1:T(8,128)}), f32[384,48]{0,1:T(8,128)}) %reduce-scatter.14.cloned.1.call-update) | async-done | bytes 73744 | tf_op jit(solution)/shard_map/reduce_scatter | solution.py:364
  1173.5 138.4 %reduce-scatter.12.cloned.1.call-done = f32[48,3,384]{2,0,1:T(8,128)} async-done(((f32[768,3,384]{2,0,1:T(8,128)}), f32[48,3,384]{2,0,1:T(8,128)}) %reduce-scatter.12.cloned.1.call-update) | async-done | bytes 221200 | tf_op jit(solution)/shard_map/reduce_scatter | solution.py:363
  (382 shorter events, 228.5 us)
Async XLA Ops:
  7.2 12.0 copy-start
  7.2 11.0 copy-start.11
  7.2 12.0 copy-start.67
  9.8 42.6 %all-to-all-start.1 = ((bf16[16,48,1024]{2,1,0:T(8,128)(2,1)}), bf16[16,48,1024]{2,1,0:T(8,128)(2,1)}, u32[]{:S(2)}, u32[]{:S(2)}) async-start(bf16[16,48,1024]{2,1,0:T(8,128)(2,1)} %bitcast.213), calls=%async_computation.1 | async-start | bytes 3145728 | tf_op jit(solution)/shard_map/all_to_all | solution.py:100
  28.3 34.7 %copy-start.30 = (s32[1024]{0:T(1024)S(1)}, s32[1024]{0:T(1024)}, u32[]{:S(2)}) copy-start(s32[1024]{0:T(1024)} %param.34) | copy-start | bytes 12292
  54.9 51.8 %all-to-all-start.2 = ((bf16[16,48,1024]{2,1,0:T(8,128)(2,1)}), bf16[16,48,1024]{2,1,0:T(8,128)(2,1)}, u32[]{:S(2)}, u32[]{:S(2)}) async-start(bf16[16,48,1024]{2,1,0:T(8,128)(2,1)} %bitcast.211), calls=%async_computation.2 | async-start | bytes 3145728 | tf_op jit(solution)/shard_map/all_to_all | solution.py:103
  62.6 74.4 %all-reduce.12.cloned.1.call-start = ((), (), s32[]{:S(2)}) async-start(), calls=%async_computation.15 | async-start | bytes 6291456 | tf_op jit(solution)/shard_map/psum | solution.py:154
  99.7 6.3 copy-start.3
  99.7 6.3 copy-start.6
  99.7 6.3 copy-start.40
  108.4 28.6 %copy-start.12 = (bf16[1024,768]{1,0:T(8,128)(2,1)S(1)}, bf16[1024,768]{1,0:T(8,128)(2,1)}, u32[]{:S(2)}) copy-start(bf16[1024,768]{1,0:T(8,128)(2,1)} %param.21) | copy-start | bytes 4718596
  108.4 40.5 %all-to-all-start.3 = ((bf16[16,48,1024]{2,1,0:T(8,128)(2,1)}), bf16[16,48,1024]{2,1,0:T(8,128)(2,1)}, u32[]{:S(2)}, u32[]{:S(2)}) async-start(bf16[16,48,1024]{2,1,0:T(8,128)(2,1)} %bitcast.212), calls=%async_computation.3 | async-start | bytes 3145728 | tf_op jit(solution)/shard_map/all_to_all | solution.py:106
  124.1 195.9 %copy-start.57 = (pred[1024,2]{0,1:T(4,128)(4,1)}, pred[1024,2]{0,1:T(4,128)(4,1)S(1)}, u32[]{:S(2)}) copy-start(pred[1024,2]{0,1:T(4,128)(4,1)S(1)} %get-tuple-element.298) | copy-start | bytes 6148
  128.8 8.1 copy-start.61
  148.9 7.4 copy-start.16
  148.9 50.9 %all-to-all-start = ((bf16[16,88,768]{2,1,0:T(8,128)(2,1)}), bf16[16,88,768]{2,1,0:T(8,128)(2,1)}, u32[]{:S(2)}, u32[]{:S(2)}) async-start(bf16[16,88,768]{2,1,0:T(8,128)(2,1)} %bitcast.207), calls=%async_computation | async-start | bytes 4325376 | tf_op jit(solution)/shard_map/all_to_all | solution.py:179
  160.6 8.6 copy-start.15
  160.6 8.6 copy-start.42
  160.6 8.6 copy-start.63
  160.6 9.8 copy-start.49
  199.9 53.2 %all-to-all-start.5 = ((bf16[16,88,768]{2,1,0:T(8,128)(2,1)}), bf16[16,88,768]{2,1,0:T(8,128)(2,1)}, u32[]{:S(2)}, u32[]{:S(2)}) async-start(bf16[16,88,768]{2,1,0:T(8,128)(2,1)} %bitcast.208), calls=%async_computation.5 | async-start | bytes 4325376 | tf_op jit(solution)/shard_map/all_to_all | solution.py:233
  209.8 101.2 %all-reduce.16.cloned.1.call-start = ((), (), s32[]{:S(2)}) async-start(), calls=%async_computation.22 | async-start | bytes 8650752 | tf_op jit(solution)/shard_map/psum | solution.py:184
  262.0 10.4 copy-start.78
  277.7 40.3 %copy-start.17 = (bf16[1024,768]{1,0:T(8,128)(2,1)S(1)}, bf16[1024,768]{1,0:T(8,128)(2,1)}, u32[]{:S(2)}) copy-start(bf16[1024,768]{1,0:T(8,128)(2,1)} %param.37) | copy-start | bytes 4718596
  311.0 51.4 %all-to-all-start.4 = ((bf16[16,88,768]{2,1,0:T(8,128)(2,1)}), bf16[16,88,768]{2,1,0:T(8,128)(2,1)}, u32[]{:S(2)}, u32[]{:S(2)}) async-start(bf16[16,88,768]{2,1,0:T(8,128)(2,1)} %get-tuple-element.259), calls=%async_computation.4 | async-start | bytes 4325376 | tf_op jit(solution)/shard_map/all_to_all | solution.py:185
  362.4 86.9 %all-to-all-start.6 = ((bf16[16,88,768]{2,1,0:T(8,128)(2,1)}), bf16[16,88,768]{2,1,0:T(8,128)(2,1)}, u32[]{:S(2)}, u32[]{:S(2)}) async-start(bf16[16,88,768]{2,1,0:T(8,128)(2,1)} %get-tuple-element.260), calls=%async_computation.6 | async-start | bytes 4325376 | tf_op jit(solution)/shard_map/all_to_all | solution.py:260
  373.4 449.0 %reduce-scatter.20.cloned.1.call-start = ((), (), s32[]{:S(2)}) async-start(), calls=%async_computation.21 | async-start | bytes 417792
  388.9 7.8 copy-start.66
  396.7 48.4 %copy-start.58 = (pred[1024,2]{0,1:T(4,128)(4,1)S(1)}, pred[1024,2]{0,1:T(4,128)(4,1)}, u32[]{:S(2)}) copy-start(pred[1024,2]{0,1:T(4,128)(4,1)} %copy-done.57) | copy-start | bytes 6148
  445.9 18.4 %copy-start.39 = (f32[1024,12]{0,1:T(8,128)}, f32[1024,12]{0,1:T(8,128)S(1)}, u32[]{:S(2)}) copy-start(f32[1024,12]{0,1:T(8,128)S(1)} %select_reduce_fusion) | copy-start | bytes 147460
  446.0 39.1 %copy-start.36 = (bf16[1024,12]{0,1:T(8,128)(2,1)}, bf16[1024,12]{0,1:T(8,128)(2,1)S(1)}, u32[]{:S(2)}) copy-start(bf16[1024,12]{0,1:T(8,128)(2,1)S(1)} %convert.51) | copy-start | bytes 73732
  472.3 12.0 copy-start.51
  472.4 12.0 copy-start.52
  472.4 12.8 copy-start.54
  472.4 12.8 copy-start.60
  472.4 12.7 copy-start.64
  472.4 12.7 copy-start.72
  485.1 5.7 copy-start.43
  485.1 5.6 copy-start.8
  496.2 129.4 %copy-start.65 = (f32[2,768]{1,0:T(2,128)S(1)}, f32[2,768]{1,0:T(2,128)}, u32[]{:S(2)}) copy-start(f32[2,768]{1,0:T(2,128)} %get-tuple-element.205) | copy-start | bytes 18436
  496.2 130.5 %copy-start.37 = (bf16[1024,12]{0,1:T(8,128)(2,1)S(1)}, bf16[1024,12]{0,1:T(8,128)(2,1)}, u32[]{:S(2)}) copy-start(bf16[1024,12]{0,1:T(8,128)(2,1)} %copy-done.36) | copy-start | bytes 73732
  508.5 11.7 slice-start
  508.5 11.7 slice-start.1
  508.5 13.0 slice-start.2
  572.6 11.7 slice-start
  572.6 11.7 slice-start.1
  572.6 13.0 slice-start.2
  611.8 5.8 copy-start.20
  625.7 7.3 copy-start.5
  625.7 7.3 copy-start.28
  626.6 269.1 %reduce-scatter.18.cloned.1.call-start = ((), (), s32[]{:S(2)}) async-start(), calls=%async_computation.20 | async-start | bytes 417792
  632.9 388.0 %reduce-scatter.16.cloned.1.call-start = ((), (), s32[]{:S(2)}) async-start(), calls=%async_computation.19 | async-start | bytes 417792
  641.1 402.2 %all-reduce.14.cloned.1.call-start = ((), (), s32[]{:S(2)}) async-start(), calls=%async_computation.16 | async-start | bytes 3145728 | tf_op jit(solution)/shard_map/psum | solution.py:354
  646.0 527.5 %reduce-scatter.14.cloned.1.call-start = ((), (), s32[]{:S(2)}) async-start(), calls=%async_computation.18 | async-start | bytes 1253376 | tf_op jit(solution)/shard_map/reduce_scatter | solution.py:364
  672.7 12.1 copy-start.13
  672.7 12.1 copy-start.56
  672.7 12.1 copy-start.68
  677.8 40.2 %all-to-all-start.9 = ((bf16[16,2,24576]{2,1,0:T(2,128)(2,1)}), bf16[16,2,24576]{2,1,0:T(2,128)(2,1)}, u32[]{:S(2)}, u32[]{:S(2)}) async-start(bf16[16,2,24576]{2,1,0:T(2,128)(2,1)} %reshape.754), calls=%async_computation.11 | async-start | bytes 3145728 | tf_op jit(solution)/shard_map/all_to_all | solution.py:290
  684.7 627.1 %reduce-scatter.12.cloned.1.call-start = ((), (), s32[]{:S(2)}) async-start(), calls=%async_computation.17 | async-start | bytes 3760128 | tf_op jit(solution)/shard_map/reduce_scatter | solution.py:363
  718.0 42.1 %all-to-all-start.7 = ((bf16[16,2,24576]{2,1,0:T(2,128)(2,1)}), bf16[16,2,24576]{2,1,0:T(2,128)(2,1)}, u32[]{:S(2)}, u32[]{:S(2)}) async-start(bf16[16,2,24576]{2,1,0:T(2,128)(2,1)} %reshape.750), calls=%async_computation.9 | async-start | bytes 3145728 | tf_op jit(solution)/shard_map/all_to_all | solution.py:276
  747.1 20.3 %copy-start.77 = (u32[32]{0:T(128)S(1)}, u32[32]{0:T(128)}, u32[]{:S(2)}) copy-start(u32[32]{0:T(128)} %constant.130) | copy-start | bytes 388
  760.1 44.3 %all-to-all-start.8 = ((bf16[16,2,24576]{2,1,0:T(2,128)(2,1)}), bf16[16,2,24576]{2,1,0:T(2,128)(2,1)}, u32[]{:S(2)}, u32[]{:S(2)}) async-start(bf16[16,2,24576]{2,1,0:T(2,128)(2,1)} %reshape.752), calls=%async_computation.10 | async-start | bytes 3145728 | tf_op jit(solution)/shard_map/all_to_all | solution.py:283
  818.8 227.3 %copy-start.73 = (f32[768]{0:T(1024)S(1)}, f32[768]{0:T(1024)}, u32[]{:S(2)}) copy-start(f32[768]{0:T(1024)} %get-tuple-element.201) | copy-start | bytes 9220
  818.8 271.1 %copy-start.69 = (f32[1024]{0:T(1024)S(1)}, f32[1024]{0:T(1024)}, u32[]{:S(2)}) copy-start(f32[1024]{0:T(1024)} %get-tuple-element.306) | copy-start | bytes 12292
  (47 other events, 150.3 us)
Sparse Core Ops, SparseCore 0:
  106.1 24.4 all-reduce.11
  277.9 33.1 all-reduce.15
  626.8 135.5 reduce-scatter.19
  767.6 128.0 reduce-scatter.17
  900.2 120.6 reduce-scatter.15
  1023.8 19.4 all-reduce.13
  1048.6 124.7 reduce-scatter.13
  1179.1 132.6 reduce-scatter.11
where the time goes:
time: 1340 us; the launch traced here: 1320 us
  waiting for transfers between devices  547 us (41%)
  local copies, waits for them, and re-layouts  274 us (20%)
  other arithmetic  178 us (13%)
  matrix products  172 us (13%)
  starting transfers between devices  81.4 us (6%)
  blocking collectives  42.7 us (3%)
  between operations  16.1 us (1%)
    unnamed x11, waiting for transfers between devices  196 us
    reduce_scatter x1, waiting for transfers between devices, local(): lax.psum_scatter(grad_qkv, 'expert', scatter_dimension=0, tiled=True)  138 us
    unnamed x175, local copies, waits for them, and re-layouts  82 us
    reduce_scatter x1, waiting for transfers between devices, local(): lax.psum_scatter(grad_wout, 'expert', scatter_dimension=1, tiled=True)  79.7 us
    reduce_sum x1, other arithmetic, local(): grad_cvec = jnp.sum(mixing[:, :, 1:2] * const_grad, axis=0)  47.2 us
    unnamed x1, blocking collectives  42.7 us
    unnamed x5, other arithmetic  37.9 us
    dynamic_update_slice x4, local copies, waits for them, and re-layouts, local(): contexts, log_totals = lax.map(forward_block, jnp.arange(block_count))  33.5 us
  transfers between devices with their start and end apart: 18, of which 12 were waited for; matrix products, arithmetic and copies ran while one was open for 31% of the time, Pallas kernels for 0%

commit v1 on v0

v1 whole, which is shorter than its diff:
```python
import functools

import jax
import jax.numpy as jnp
import numpy as np
from jax import lax
from jax.experimental import pallas as pl
from jax.experimental.pallas import tpu as pltpu
from jax.sharding import PartitionSpec as P

HD = 64
CAP = 176
PARTS = 2
EPSILON = 1e-06
BF = jnp.bfloat16
F32 = jnp.float32
NEG = -1e30
VMEM_LIMIT = 56 * 1024 * 1024


def nn(a, b):
    return lax.dot_general(a, b, (((1,), (0,)), ((), ())), preferred_element_type=F32)


def nt(a, b):
    return lax.dot_general(a, b, (((1,), (1,)), ((), ())), preferred_element_type=F32)


def tn(a, b):
    return lax.dot_general(a, b, (((0,), (0,)), ((), ())), preferred_element_type=F32)


def iota(shape, dim):
    return lax.broadcasted_iota(jnp.int32, shape, dim)


def params(**kw):
    return pltpu.CompilerParams(vmem_limit_bytes=VMEM_LIMIT, **kw)


def cost(flops, nbytes, trans=0):
    return pl.CostEstimate(flops=int(flops), bytes_accessed=int(nbytes), transcendentals=int(trans))


def whole(shape):
    return pl.BlockSpec(shape, lambda *_: (0,) * len(shape))


SMEM = pl.BlockSpec(memory_space=pltpu.SMEM)


def swap_halves(values):
    width = values.shape[1]
    half = HD // 2
    lane = iota(values.shape, 1)
    ahead = pltpu.roll(values, width - half, 1)
    behind = pltpu.roll(values, half, 1)
    return jnp.where(lax.rem(lane, HD) < half, ahead, behind)


def qkv_body(h_ref, gain_ref, w_ref, cos_ref, sin_ref, n_ref, q_ref, k_ref, v_ref):
    h = h_ref[...].astype(F32)
    inv = lax.rsqrt(jnp.mean(h * h, axis=-1, keepdims=True) + EPSILON)
    normed = (h * inv * gain_ref[...]).astype(BF)
    n_ref[...] = normed
    copies = q_ref.shape[1] // 128
    cos = jnp.concatenate([cos_ref[...]] * copies, axis=1)
    sin = jnp.concatenate([sin_ref[...]] * copies, axis=1)
    q = nn(normed, w_ref[0])
    q_ref[...] = ((q * cos + swap_halves(q) * sin) * (HD**-0.5)).astype(BF)
    k = nn(normed, w_ref[1])
    k_ref[...] = (k * cos + swap_halves(k) * sin).astype(BF)
    v_ref[...] = nn(normed, w_ref[2]).astype(BF)


def qkv(hidden, gain, w3, cos, sin):
    length, width = hidden.shape
    inner = w3.shape[2]
    blk = 256
    row = lambda n: pl.BlockSpec((blk, n), lambda i: (i, 0))
    return pl.pallas_call(
        qkv_body,
        grid=(length // blk,),
        in_specs=[row(width), whole((1, width)), whole(w3.shape), row(128), row(128)],
        out_specs=[row(width), row(inner), row(inner), row(inner)],
        out_shape=[jax.ShapeDtypeStruct((length, width), BF)]
        + [jax.ShapeDtypeStruct((length, inner), BF)] * 3,
        compiler_params=params(),
        cost_estimate=cost(2 * length * width * inner * 3, 10 << 20),
        name="qkv",
    )(hidden, gain, w3, cos, sin)


def document_of(position, meta_ref):
    doc = jnp.zeros(position.shape, jnp.int32)
    for j in range(3):
        doc = doc + (position >= meta_ref[4 + j]).astype(jnp.int32)
    return doc


def span_of(position, meta_ref):
    span = jnp.zeros(position.shape, jnp.int32)
    for j in range(PARTS):
        inside = (position >= meta_ref[j]) & (position < meta_ref[2 + j])
        span = jnp.where(inside, span + (j + 1), span)
    return span


def mask_bias(query_pos, key_pos, meta_ref):
    query_span = span_of(query_pos, meta_ref)
    query_span = jnp.where(query_span == 0, -1, query_span)
    key_span = span_of(key_pos, meta_ref)
    same_doc = document_of(query_pos, meta_ref) == document_of(key_pos, meta_ref)
    seen = same_doc & ((key_pos <= query_pos) | (query_span == key_span))
    return jnp.where(seen, 0.0, NEG)


def attend_body(meta_ref, q_ref, k_ref, v_ref, ctx_ref, lse_ref, bias_ref):
    block = pl.program_id(0)
    pair = pl.program_id(1)
    rows, total = bias_ref.shape
    chunk = 256

    def run(keys):
        @pl.when(pair == 0)
        def _():
            for c in range(rows // chunk):
                qpos = block * rows + c * chunk + iota((chunk, 1), 0)
                kpos = iota((1, keys), 1)
                bias_ref[c * chunk : (c + 1) * chunk, :keys] = mask_bias(qpos, kpos, meta_ref)

        lane = iota((1, 128), 1)

        def step(c, carry):
            at = pl.multiple_of(c * chunk, chunk)
            q = q_ref[pl.ds(at, chunk), :]
            bias = bias_ref[pl.ds(at, chunk), :keys]
            k = k_ref[:keys, :]
            v = v_ref[:keys, :]
            outs = []
            for head in range(2):
                own = (lane // HD) == head
                qh = jnp.where(own, q, jnp.zeros_like(q))
                s = nt(qh, k) + bias
                top = jnp.max(s, axis=-1, keepdims=True)
                p = jnp.exp(s - top).astype(BF)
                mixed = nn(p, jnp.where(own, v, jnp.ones_like(v)))
                norm = pltpu.roll(mixed, HD, 1)
                outs.append((mixed / norm, top + jnp.log(norm)))
            first = lane < HD
            ctx_ref[pl.ds(at, chunk), :] = jnp.where(first, outs[0][0], outs[1][0]).astype(BF)
            lse = jnp.where(first, outs[0][1], outs[1][1]).T
            at2 = pl.multiple_of(block * rows + c * chunk, chunk)
            lse_ref[pl.ds(2 * pair, 1), pl.ds(at2, chunk)] = lse[0:1]
            lse_ref[pl.ds(2 * pair + 1, 1), pl.ds(at2, chunk)] = lse[HD : HD + 1]
            return carry

        lax.fori_loop(0, rows // chunk, step, 0)

    for b in range(PARTS):

        @pl.when(block == b)
        def _(b=b):
            run((b + 1) * rows)


def attend(meta, q, k, v):
    length, inner = q.shape
    pairs = inner // 128
    rows = length // PARTS
    heads8 = 8 * ((2 * pairs + 7) // 8)
    return pl.pallas_call(
        attend_body,
        grid=(PARTS, pairs),
        in_specs=[
            SMEM,
            pl.BlockSpec((rows, 128), lambda b, p: (b, p)),
            pl.BlockSpec((length, 128), lambda b, p: (0, p)),
            pl.BlockSpec((length, 128), lambda b, p: (0, p)),
        ],
        out_specs=[
            pl.BlockSpec((rows, 128), lambda b, p: (b, p)),
            whole((heads8, length)),
        ],
        out_shape=[
            jax.ShapeDtypeStruct((length, inner), BF),
            jax.ShapeDtypeStruct((heads8, length), F32),
        ],
        scratch_shapes=[pltpu.VMEM((rows, length), F32)],
        compiler_params=params(),
        cost_estimate=cost(4 * length * length * inner, 8 << 20, length * length * 6),
        name="attend",
    )(meta, q, k, v)


def attend_back_body(
    meta_ref, q_ref, k_ref, v_ref, ctx_ref, lse_ref, ag_ref, wo_ref, cos_ref, sin_ref,
    pq_ref, pk_ref, pv_ref, bias_ref, do_ref, delta_ref, dq0_ref, dq1_ref, sl_ref,
):
    pair = pl.program_id(0)
    length = q_ref.shape[0]
    rows = length // PARTS
    chunk = 256
    lane = iota((1, 128), 1)
    first = lane < HD

    @pl.when(pair == 0)
    def _():
        def fill(c, carry):
            at = pl.multiple_of(c * chunk, chunk)
            kpos = at + iota((chunk, 1), 0)
            qpos = iota((1, length), 1)
            bias_ref[pl.ds(at, chunk), :] = mask_bias(qpos, kpos, meta_ref)
            return carry

        lax.fori_loop(0, length // chunk, fill, 0)

    def prepare(c, carry):
        at = pl.multiple_of(c * chunk, chunk)
        grad = nt(ag_ref[pl.ds(at, chunk), :], wo_ref[...]).astype(BF)
        do_ref[pl.ds(at, chunk), :] = grad
        prod = (grad.astype(F32) * ctx_ref[pl.ds(at, chunk), :].astype(F32)).T
        delta_ref[0:1, pl.ds(at, chunk)] = jnp.sum(prod[:HD], axis=0, keepdims=True)
        delta_ref[1:2, pl.ds(at, chunk)] = jnp.sum(prod[HD:], axis=0, keepdims=True)
        return carry

    lax.fori_loop(0, length // chunk, prepare, 0)
    dq0_ref[...] = jnp.zeros_like(dq0_ref)
    dq1_ref[...] = jnp.zeros_like(dq1_ref)

    def step(c, carry, start):
        count = length - start
        at = pl.multiple_of(c * chunk, chunk)
        k = k_ref[pl.ds(at, chunk), :]
        v = v_ref[pl.ds(at, chunk), :]
        bias = bias_ref[pl.ds(at, chunk), start:]
        q = q_ref[start:, :]
        grad = do_ref[start:, :]
        dks = []
        dvs = []
        for head in range(2):
            own = (lane // HD) == head
            kh = jnp.where(own, k, jnp.zeros_like(k))
            vh = jnp.where(own, v, jnp.zeros_like(v))
            lse = lse_ref[pl.ds(2 * pair + head, 1), start:]
            p = jnp.exp(nt(kh, q) + bias - lse)
            dvs.append(nn(p.astype(BF), grad))
            dp = nt(vh, grad)
            ds = (p * (dp - delta_ref[head : head + 1, start:])).astype(BF)
            dks.append(nn(ds, q))
            dq_ref = dq0_ref if head == 0 else dq1_ref
            dq_ref[start:, :] += tn(ds, k)
        dk = jnp.where(first, dks[0], dks[1])
        cos = cos_ref[pl.ds(at, chunk), :]
        sin = sin_ref[pl.ds(at, chunk), :]
        pk_ref[pl.ds(at, chunk), :] = (dk * cos - swap_halves(dk) * sin).astype(BF)
        pv_ref[pl.ds(at, chunk), :] = jnp.where(first, dvs[0], dvs[1]).astype(BF)
        return carry

    for b in range(PARTS):
        per = rows // chunk
        lax.fori_loop(b * per, (b + 1) * per, functools.partial(step, start=b * rows), 0)

    def finish(c, carry):
        at = pl.multiple_of(c * chunk, chunk)
        dq = jnp.where(first, dq0_ref[pl.ds(at, chunk), :], dq1_ref[pl.ds(at, chunk), :])
        dq = dq * (HD**-0.5)
        cos = cos_ref[pl.ds(at, chunk), :]
        sin = sin_ref[pl.ds(at, chunk), :]
        pq_ref[pl.ds(at, chunk), :] = (dq * cos - swap_halves(dq) * sin).astype(BF)
        return carry

    lax.fori_loop(0, length // chunk, finish, 0)


def attend_back(meta, q, k, v, ctx, lse, agrad, w_out, cos, sin):
    length, inner = q.shape
    width = agrad.shape[1]
    pairs = inner // 128
    col = pl.BlockSpec((length, 128), lambda p: (0, p))
    return pl.pallas_call(
        attend_back_body,
        grid=(pairs,),
        in_specs=[
            SMEM, col, col, col, col, whole(lse.shape), whole((length, width)),
            pl.BlockSpec((128, width), lambda p: (p, 0)),
            whole((length, 128)), whole((length, 128)),
        ],
        out_specs=[col, col, col],
        out_shape=[jax.ShapeDtypeStruct((length, inner), BF)] * 3,
        scratch_shapes=[
            pltpu.VMEM((length, length), F32),
            pltpu.VMEM((length, 128), BF),
            pltpu.VMEM((8, length), F32),
            pltpu.VMEM((length, 128), F32),
            pltpu.VMEM((length, 128), F32),
            pltpu.VMEM((8, 128), F32),
        ],
        compiler_params=params(),
        cost_estimate=cost(10 * length * length * inner, 12 << 20, length * length * 6),
        name="attend_back",
    )(meta, q, k, v, ctx, lse, agrad, w_out, cos, sin)


def mid_body(
    tid_ref, h_ref, a_ref, b_ref, gain_ref, joint_ref, prev_ref, routes_ref, og_ref,
    r_ref, n_ref, send_ref, rows_ref, cols_ref, lg_ref, col_ref,
):
    length = h_ref.shape[0]
    width = h_ref.shape[1]
    routes_total = prev_ref.shape[0]
    experts = routes_total - 4
    half = CAP // 2
    slots = send_ref.shape[0]
    chunk = 256
    tid = tid_ref[0]

    def norm(c, carry):
        at = pl.multiple_of(c * chunk, chunk)
        r = h_ref[pl.ds(at, chunk), :].astype(F32) + (
            a_ref[pl.ds(at, chunk), :] + b_ref[pl.ds(at, chunk), :]
        )
        r_ref[pl.ds(at, chunk), :] = r
        inv = lax.rsqrt(jnp.mean(r * r, axis=-1, keepdims=True) + EPSILON)
        normed = (r * inv * gain_ref[...]).astype(BF)
        n_ref[pl.ds(at, chunk), :] = normed
        lg_ref[:, pl.ds(at, chunk)] = nt(joint_ref[...], normed)
        return carry

    lax.fori_loop(0, length // chunk, norm, 0)

    lg = lg_ref[...]
    logits = lg[:routes_total] + prev_ref[...]
    route = [routes_ref[k : k + 1, :] for k in range(2)]
    rid = iota((routes_total, length), 0)
    chosen = [jnp.sum(jnp.where(rid == r, logits, 0.0), axis=0, keepdims=True) for r in route]
    top = jnp.maximum(chosen[0], chosen[1])
    raised = [jnp.exp(c - top) for c in chosen]
    total = raised[0] + raised[1]
    gate = [e / total for e in raised]

    rid16 = iota((16, length), 0)
    hot = ((rid16 == route[0]) | (rid16 == route[1])).astype(F32)
    blk = 256
    upper = (iota((blk, blk), 0) < iota((blk, blk), 1)).astype(BF)
    before = jnp.zeros((16, 1), F32)
    parts = []
    for c in range(length // blk):
        part = hot[:, c * blk : (c + 1) * blk]
        parts.append(nn(part.astype(BF), upper) + before)
        before = before + jnp.sum(part, axis=1, keepdims=True)
    count = jnp.concatenate(parts, axis=1)
    column = []
    for k in range(2):
        pos = jnp.sum(jnp.where(rid16 == route[k], count, 0.0), axis=0, keepdims=True)
        pos = pos.astype(jnp.int32)
        kept = (route[k] < experts) & (pos < CAP)
        side = (pos >= half).astype(jnp.int32)
        col = jnp.where(side == tid, 0, slots) + route[k] * half + pos - side * half
        column.append(jnp.where(kept, col, -1))
    mix = []
    for j in range(2):
        c0 = lg[routes_total + 2 * j : routes_total + 2 * j + 1]
        c1 = lg[routes_total + 2 * j + 1 : routes_total + 2 * j + 2]
        peak = jnp.maximum(c0, c1)
        e0 = jnp.exp(c0 - peak)
        e1 = jnp.exp(c1 - peak)
        mix.append((e0 / (e0 + e1), e1 / (e0 + e1)))
    rows_ref[...] = jnp.zeros_like(rows_ref)

    def put(i, value):
        rows_ref[i : i + 1, :] = value

    for k in range(2):
        put(k, gate[k])
        put(2 + k, column[k].astype(F32))
        copy = (route[k] == experts + 1).astype(F32)
        con = [(route[k] == experts + 2 + j).astype(F32) for j in range(2)]
        put(4 + k, copy + con[0] * mix[0][0] + con[1] * mix[1][0])
        put(6 + 2 * k, con[0] * mix[0][1])
        put(7 + 2 * k, con[1] * mix[1][1])
        put(10 + 2 * k, mix[k][0])
        put(11 + 2 * k, mix[k][1])
        put(14 + k, route[k].astype(F32))
    col_ref[...] = jnp.zeros_like(col_ref)
    col_ref[0:16, :] = rows_ref[...]

    def turn(c, carry):
        at = pl.multiple_of(c * chunk, chunk)
        cols_ref[pl.ds(at, chunk), :] = col_ref[:, pl.ds(at, chunk)].T
        return carry

    lax.fori_loop(0, length // chunk, turn, 0)

    piece = 176

    def dispatch(c, carry):
        at = pl.multiple_of(c * piece, 16)
        slot = at + iota((piece, 1), 0)
        col0 = rows_ref[2:3, :].astype(jnp.int32)
        col1 = rows_ref[3:4, :].astype(jnp.int32)
        m0 = slot == col0
        m1 = slot == col1
        pick = jnp.where(m0 | m1, 1.0, 0.0).astype(BF)
        weight = jnp.sum(
            jnp.where(m0, rows_ref[0:1, :], 0.0) + jnp.where(m1, rows_ref[1:2, :], 0.0),
            axis=1,
            keepdims=True,
        )
        send_ref[pl.ds(at, piece), :width] = nn(pick, n_ref[...]).astype(BF)
        send_ref[pl.ds(at, piece), width:] = (nn(pick, og_ref[...]) * weight).astype(BF)
        return carry

    lax.fori_loop(0, slots // piece, dispatch, 0)


def mid(tid, hidden, mine, other, gain, joint, prev, routes, og):
    length, width = hidden.shape
    experts = prev.shape[0] - 4
    slots = experts * (CAP // 2)
    return pl.pallas_call(
        mid_body,
        in_specs=[SMEM] + [pl.BlockSpec(memory_space=pltpu.VMEM)] * 8,
        out_specs=[pl.BlockSpec(memory_space=pltpu.VMEM)] * 5,
        out_shape=[
            jax.ShapeDtypeStruct((length, width), F32),
            jax.ShapeDtypeStruct((length, width), BF),
            jax.ShapeDtypeStruct((slots, 2 * width), BF),
            jax.ShapeDtypeStruct((16, length), F32),
            jax.ShapeDtypeStruct((length, 128), F32),
        ],
        scratch_shapes=[pltpu.VMEM((16, length), F32), pltpu.VMEM((128, length), F32)],
        compiler_params=params(),
        cost_estimate=cost(4 * slots * length * width, 16 << 20),
        name="mid",
    )(tid, hidden, mine, other, gain, joint, prev, routes, og)


def expert_body(
    own_ref, oth_ref, wg_ref, wu_ref, wd_ref, yown_ref, yoth_ref, grad_ref,
    x_ref, hid_ref, gp_ref, up_ref, xt_ref, dt_ref, y_ref,
):
    half = own_ref.shape[0]
    width = own_ref.shape[1] // 2
    units = hid_ref.shape[1]
    slots = 2 * half
    x_ref[:half, :] = own_ref[...]
    x_ref[half:, :] = oth_ref[...]
    w_gate = wg_ref[...].reshape(width, units)
    w_up = wu_ref[...].reshape(width, units)
    w_down = wd_ref[...].reshape(width, units)
    piece = 352

    def forward(c, carry):
        at = pl.multiple_of(c * piece, 16)
        x = x_ref[pl.ds(at, piece), :width]
        dy = x_ref[pl.ds(at, piece), width:]
        gate = nn(x, w_gate)
        up = nn(x, w_up)
        hg = nn(dy, w_down)
        sig = jax.nn.sigmoid(gate)
        act = gate * sig
        hid = (act * up).astype(BF)
        gp = (hg * up * sig * (1.0 + gate * (1.0 - sig))).astype(BF)
        upg = (hg * act).astype(BF)
        hid_ref[pl.ds(at, piece), :] = hid
        gp_ref[pl.ds(at, piece), :] = gp
        up_ref[pl.ds(at, piece), :] = upg
        y_ref[pl.ds(at, piece), :width] = nt(hid, w_down).astype(BF)
        y_ref[pl.ds(at, piece), width:] = (nt(gp, w_gate) + nt(upg, w_up)).astype(BF)
        return carry

    lax.fori_loop(0, slots // piece, forward, 0)
    yown_ref[...] = y_ref[:half, :]
    yoth_ref[...] = y_ref[half:, :]

    def turn(c, carry):
        at = pl.multiple_of(c * 128, 128)
        xt_ref[:, pl.ds(at, 128)] = x_ref[pl.ds(at, 128), :width].T
        dt_ref[:, pl.ds(at, 128)] = x_ref[pl.ds(at, 128), width:].T
        return carry

    lax.fori_loop(0, slots // 128, turn, 0)
    tile = 256
    peers, three, share, _ = grad_ref.shape
    for m, (left, right) in enumerate(((xt_ref, gp_ref), (xt_ref, up_ref), (dt_ref, hid_ref))):

        def weight(c, carry, m=m, left=left, right=right):
            at = pl.multiple_of(c * tile, tile)
            value = nn(left[...], right[:, pl.ds(at, tile)]).astype(BF)
            grad_ref[:, m, :, pl.ds(at, tile)] = value.reshape(peers, share, tile)
            return carry

        lax.fori_loop(0, units // tile, weight, 0)


def experts_call(own, oth, weights):
    half, twice = own.shape
    peers, three, share, units = weights.shape
    width = twice // 2
    slots = 2 * half
    third = lambda m: pl.BlockSpec((peers, None, share, units), lambda i, m=m: (0, m, 0, 0))
    return pl.pallas_call(
        expert_body,
        grid=(1,),
        in_specs=[whole(own.shape), whole(oth.shape), third(0), third(1), third(2)],
        out_specs=[whole(own.shape), whole(own.shape), whole(weights.shape)],
        out_shape=[
            jax.ShapeDtypeStruct(own.shape, BF),
            jax.ShapeDtypeStruct(own.shape, BF),
            jax.ShapeDtypeStruct(weights.shape, BF),
        ],
        scratch_shapes=[
            pltpu.VMEM((slots, twice), BF),
            pltpu.VMEM((slots, units), BF),
            pltpu.VMEM((slots, units), BF),
            pltpu.VMEM((slots, units), BF),
            pltpu.VMEM((width, slots), BF),
            pltpu.VMEM((width, slots), BF),
            pltpu.VMEM((slots, twice), BF),
        ],
        compiler_params=params(),
        cost_estimate=cost(18 * slots * width * units, 22 << 20),
        name="experts",
    )(own, oth, weights, weights, weights)


def combine_body(
    own_ref, oth_ref, r_ref, n_ref, rows_ref, cols_ref, gain_ref, cvec_ref, joint_ref, og_ref,
    out_ref, prev_ref, rg_ref, ag_ref, small_ref,
    y_ref, fs_ref, red_ref, jg_ref, jf_ref,
):
    length, width = r_ref.shape
    half = own_ref.shape[0]
    routes_total = prev_ref.shape[0]
    experts = routes_total - 4
    chunk = 256
    y_ref[:half, :] = own_ref[...]
    y_ref[half:, :] = oth_ref[...]
    gain = gain_ref[...]
    cvec = [cvec_ref[j : j + 1, :] for j in range(2)]
    red_ref[...] = jnp.zeros_like(red_ref)

    def first(c, carry):
        at = pl.multiple_of(c * chunk, chunk)
        cols = cols_ref[pl.ds(at, chunk), :]
        col = lambda i: cols[:, i : i + 1]
        slot = iota((1, 2 * half), 1)
        p0 = jnp.where(slot == col(2).astype(jnp.int32), 1.0, 0.0)
        p1 = jnp.where(slot == col(3).astype(jnp.int32), 1.0, 0.0)
        fs_ref[pl.ds(at, chunk), :] = nn((p0 + p1).astype(BF), y_ref[:, width:])
        got = [nn(p.astype(BF), y_ref[:, :width]) for p in (p0, p1)]
        r = r_ref[pl.ds(at, chunk), :]
        inv = lax.rsqrt(jnp.mean(r * r, axis=-1, keepdims=True) + EPSILON)
        nf = r * inv * gain
        og = og_ref[pl.ds(at, chunk), :].astype(F32)
        out = r
        sums = []
        for k in range(2):
            pair = got[k] + col(4 + k) * nf
            pair = pair + col(6 + 2 * k) * cvec[0] + col(7 + 2 * k) * cvec[1]
            out = out + col(k) * pair
            sums.append(jnp.sum(og * pair, axis=-1, keepdims=True))
        out_ref[pl.ds(at, chunk), :] = out.astype(BF)
        sums.append(jnp.sum(og * nf, axis=-1, keepdims=True))
        for j in range(2):
            sums.append(jnp.sum(og * cvec[j], axis=-1, keepdims=True))
        lane = iota((1, 128), 1)
        packed = jnp.zeros((chunk, 128), F32)
        for i, value in enumerate(sums):
            packed = jnp.where(lane == i, value, packed)
        red_ref[0:8, pl.ds(at, chunk)] = packed.T[0:8]
        return carry

    lax.fori_loop(0, length // chunk, first, 0)

    row = lambda i: rows_ref[i : i + 1, :]
    gate = [row(0), row(1)]
    route = [row(14).astype(jnp.int32), row(15).astype(jnp.int32)]
    sums = [red_ref[i : i + 1, :] for i in range(5)]
    both = gate[0] * sums[0] + gate[1] * sums[1]
    chosen = [gate[k] * (sums[k] - both) for k in range(2)]
    rid = iota((routes_total, length), 0)
    prev = jnp.where(rid == route[0], chosen[0], 0.0) + jnp.where(rid == route[1], chosen[1], 0.0)
    prev_ref[...] = prev
    jf_ref[0:routes_total, :] = prev
    weight_at = lambda r: (
        jnp.where(route[0] == r, gate[0], 0.0) + jnp.where(route[1] == r, gate[1], 0.0)
    )
    direct = weight_at(experts + 1)
    vec_rows = []
    for j in range(2):
        m0, m1 = row(10 + 2 * j), row(11 + 2 * j)
        weight = weight_at(experts + 2 + j)
        g0 = weight * sums[2]
        g1 = weight * sums[3 + j]
        mean = m0 * g0 + m1 * g1
        jf_ref[routes_total + 2 * j : routes_total + 2 * j + 1, :] = m0 * (g0 - mean)
        jf_ref[routes_total + 2 * j + 1 : routes_total + 2 * j + 2, :] = m1 * (g1 - mean)
        direct = direct + m0 * weight
        vec_rows.append(m1 * weight)
    jg_ref[...] = jf_ref[...].astype(BF)
    red_ref[8:9, :] = direct
    small_ref[...] = jnp.zeros_like(small_ref)
    small_ref[0:16, :] = nn(jg_ref[...], n_ref[...])
    vec = jnp.concatenate(vec_rows, axis=0)
    high = vec.astype(BF).astype(F32)
    lhs = jnp.concatenate([high, vec - high, jnp.zeros((12, length), F32)], axis=0).astype(BF)
    parts = nn(lhs, og_ref[...])
    small_ref[16:18, :] = parts[0:2] + parts[2:4]

    def second(c, carry):
        at = pl.multiple_of(c * chunk, chunk)
        direct = red_ref[:, pl.ds(at, chunk)].T[:, 8:9]
        og = og_ref[pl.ds(at, chunk), :].astype(F32)
        r = r_ref[pl.ds(at, chunk), :]
        inv = lax.rsqrt(jnp.mean(r * r, axis=-1, keepdims=True) + EPSILON)
        mg = fs_ref[pl.ds(at, chunk), :] + tn(jg_ref[:, pl.ds(at, chunk)], joint_ref[...])
        mg = mg + direct * og
        small_ref[18:19, :] += jnp.sum(mg * r * inv, axis=0, keepdims=True)
        scaled = mg * gain
        rg = og + inv * scaled - r * (inv * inv * inv) * jnp.mean(
            scaled * r, axis=-1, keepdims=True
        )
        rg_ref[pl.ds(at, chunk), :] = rg
        ag_ref[pl.ds(at, chunk), :] = rg.astype(BF)
        return carry

    lax.fori_loop(0, length // chunk, second, 0)


def combine(own, oth, r, n, rows, cols, gain, cvec, joint, og):
    length, width = r.shape
    routes_total = joint.shape[0] - 4
    slots = 2 * own.shape[0]
    vmem = pl.BlockSpec(memory_space=pltpu.VMEM)
    return pl.pallas_call(
        combine_body,
        in_specs=[vmem] * 10,
        out_specs=[vmem] * 5,
        out_shape=[
            jax.ShapeDtypeStruct((length, width), BF),
            jax.ShapeDtypeStruct((routes_total, length), F32),
            jax.ShapeDtypeStruct((length, width), F32),
            jax.ShapeDtypeStruct((length, width), BF),
            jax.ShapeDtypeStruct((24, width), F32),
        ],
        scratch_shapes=[
            pltpu.VMEM((slots, 2 * width), BF),
            pltpu.VMEM((length, width), F32),
            pltpu.VMEM((128, length), F32),
            pltpu.VMEM((16, length), BF),
            pltpu.VMEM((16, length), F32),
        ],
        compiler_params=params(),
        cost_estimate=cost(6 * slots * length * width, 22 << 20),
        name="combine",
    )(own, oth, r, n, rows, cols, gain, cvec, joint, og)


def final_body(h_ref, gain_ref, rg_ref, a_ref, b_ref, out_ref, grad_ref):
    @pl.when(pl.program_id(0) == 0)
    def _():
        grad_ref[...] = jnp.zeros_like(grad_ref)

    h = h_ref[...].astype(F32)
    inv = lax.rsqrt(jnp.mean(h * h, axis=-1, keepdims=True) + EPSILON)
    up = a_ref[...].astype(F32) + b_ref[...].astype(F32)
    grad_ref[0:1, :] += jnp.sum(up * h * inv, axis=0, keepdims=True)
    scaled = up * gain_ref[...]
    grad = inv * scaled - h * (inv * inv * inv) * jnp.mean(scaled * h, axis=-1, keepdims=True)
    out_ref[...] = (rg_ref[...] + grad).astype(BF)


def final(hidden, gain, rg, mine, other):
    length, width = hidden.shape
    blk = 256
    row = pl.BlockSpec((blk, width), lambda i: (i, 0))
    return pl.pallas_call(
        final_body,
        grid=(length // blk,),
        in_specs=[row, whole((1, width)), row, row, row],
        out_specs=[row, whole((8, width))],
        out_shape=[
            jax.ShapeDtypeStruct((length, width), BF),
            jax.ShapeDtypeStruct((8, width), F32),
        ],
        compiler_params=params(),
        cost_estimate=cost(20 * length * width, 9 << 20),
        name="final",
    )(hidden, gain, rg, mine, other)


def exchange(values, groups=None):
    return lax.all_to_all(
        values, "expert", split_axis=0, concat_axis=0, tiled=True, axis_index_groups=groups
    )


def swap(values):
    return lax.ppermute(values, "tensor", [(0, 1), (1, 0)])


def local(
    hidden_in, w_qkv, w_out, gain_in, gain_mid, w_router, w_const, const_vec,
    w_gate, w_up, w_down, prev_logits, routes, doc_ids, span_start, span_len, d_output,
):
    length, width = hidden_in.shape
    experts, share, units = w_gate.shape
    inner = w_qkv.shape[2]
    peers = lax.axis_size("expert")
    copies = peers // experts
    groups = [[g * experts + e for e in range(experts)] for g in range(copies)]
    routes_total = w_router.shape[1]

    stacked = jnp.stack([w_gate, w_up, w_down], axis=1).reshape(1, experts, 3 * share, units)
    sent = jnp.broadcast_to(stacked, (copies,) + stacked.shape[1:])
    weights = exchange(sent.reshape(peers, 3 * share, units)).reshape(peers, 3, share, units)
    fast = share % 16 == 0
    if not fast:
        weights = weights.transpose(1, 0, 2, 3).reshape(1, 3, width, units)

    lane = np.arange(128)
    frequency = 10000.0 ** (-jnp.asarray(lane % (HD // 2)).astype(F32) / (HD // 2))
    phase = jnp.arange(length).astype(F32)[:, None] * frequency[None, :]
    cos = jnp.cos(phase)
    sin = jnp.where((lane % HD < HD // 2)[None, :], -jnp.sin(phase), jnp.sin(phase))
    cuts = jnp.sum(doc_ids[None, :] < jnp.arange(1, 4)[:, None], axis=1, dtype=jnp.int32)
    meta = jnp.concatenate(
        [span_start[0], span_start[0] + span_len[0], cuts, jnp.zeros((1,), jnp.int32)]
    )

    w3 = w_qkv.transpose(1, 0, 2)
    normed_in, q, k, v = qkv(hidden_in, gain_in.reshape(1, width), w3, cos, sin)
    context, lse = attend(meta, q, k, v)
    attended = jnp.dot(context, w_out, preferred_element_type=F32)
    joint = jnp.concatenate([w_router.T, w_const.T], axis=0)
    tid = lax.axis_index("tensor").astype(jnp.int32).reshape(1)
    r, n, send, rows, cols = mid(
        tid, hidden_in, attended, swap(attended), gain_mid.reshape(1, width), joint,
        prev_logits.T, routes.T, d_output,
    )

    half = CAP // 2
    got = exchange(send.reshape(experts, half, 2 * width), groups).reshape(send.shape)
    y_own, y_oth, grads = experts_call(got, swap(got), weights)
    summed = y_own + swap(y_oth)
    back = exchange(summed.reshape(experts, half, 2 * width), groups).reshape(send.shape)
    if not fast:
        grads = grads.reshape(3, peers, share, units).transpose(1, 0, 2, 3)
    parted = exchange(grads.reshape(peers, 3 * share, units))

    output, prev_grad, rg, ag, small = combine(
        back, swap(back), r, n, rows, cols, gain_mid.reshape(1, width), const_vec, joint, d_output
    )
    pq, pk, pv = attend_back(meta, q, k, v, context, lse, ag, w_out, cos, sin)
    normed_grad = nt(pq, w3[0]) + nt(pk, w3[1]) + nt(pv, w3[2])
    normed_grad = normed_grad.astype(BF)
    grad_input, gain_grad = final(
        hidden_in, gain_in.reshape(1, width), rg, normed_grad, swap(normed_grad)
    )

    shared = [tn(normed_in, g).astype(BF).reshape(peers, share, inner) for g in (pq, pk, pv)]
    shared.append(tn(ag, context).astype(BF).reshape(peers, share, inner))
    shared = exchange(jnp.concatenate(shared, axis=1)).reshape(peers, 4, share, inner)
    shared = jnp.sum(shared.astype(F32), axis=0)
    small = jnp.concatenate([small[:19], gain_grad[0:1], small[20:]], axis=0)
    small = small.reshape(24, peers, share).transpose(1, 0, 2)
    small = jnp.sum(exchange(small), axis=0)

    parted = jnp.sum(
        parted.reshape(copies, experts, 3, share, units).astype(F32), axis=0
    )
    return (
        output,
        grad_input,
        prev_grad.T,
        shared[0:3].transpose(1, 0, 2),
        shared[3].T,
        small[19],
        small[18],
        small[0:routes_total].T,
        small[routes_total : routes_total + 4].T,
        small[16:18],
        parted[:, 0],
        parted[:, 1],
        parted[:, 2],
    )


def solution(mesh):
    rows = P("expert", None)
    expert_spec = P(None, "expert", "tensor")
    return jax.shard_map(
        local,
        mesh=mesh,
        in_specs=(
            rows, P(None, None, "tensor"), P("tensor", None), P(), P(), P(), P(), P(),
            expert_spec, expert_spec, expert_spec, rows, rows, P("expert"), rows, rows, rows,
        ),
        out_specs=(
            rows, rows, rows, P("expert", None, "tensor"), P("tensor", "expert"),
            P("expert"), P("expert"), rows, rows, P(None, "expert"),
            expert_spec, expert_spec, expert_spec,
        ),
        check_vma=False,
    )
```

time: 1340 us -> 451 us (0.34); the launches traced: 1320 us -> 445 us
  waiting for transfers between devices: 547 us -> 180 us
  local copies, waits for them, and re-layouts: 274 us -> 18.4 us
  matrix products: 172 us -> 10.4 us
  other arithmetic: 178 us -> 18.2 us
  Pallas kernels: 0 us -> 123 us
  starting transfers between devices: 81.4 us -> 45.4 us
  between operations: 16.1 us -> 0.95 us
    reduce_scatter x2 -> x0, waiting for transfers between devices: 218 us -> none  [the longest x1 138 us: local(): lax.psum_scatter(grad_qkv, 'expert', scatter_dimension=0, tiled=True)]
    unnamed x11 -> x0, waiting for transfers between devices: 196 us -> none
    dot_general x32 -> x8, matrix products: 172 us -> 10.4 us  [the longest x3 4.22 us: nt(): lax.dot_general(a, b, (((1,), (1,)), ((), ())), preferred_element_type=F32)]
    pallas_call x0 -> x7, Pallas kernels: none -> 123 us  [the longest x1 33.5 us: experts_call(): pl.pallas_call(expert_body, grid=(1,), in_specs=[whole(own.shape), whole(...]
    all_to_all x10 -> x5, waiting for transfers between devices: 78.8 us -> 168 us  [exchange(): lax.all_to_all(values, 'expert', split_axis=0, concat_axis=0, tiled=True,...]
    reduce_sum x18 -> x4, other arithmetic: 84 us -> 5.46 us  [the longest x1 4.24 us: local(): jnp.sum(parted.reshape(copies, experts, 3, share, units).astype(F32), axi...]
    unnamed x175 -> x40, local copies, waits for them, and re-layouts: 82 us -> 5.98 us
    psum x3 -> x0, waiting for transfers between devices: 54.3 us -> none  [the longest x1 33.3 us: local(): summed = lax.psum(partial_value.astype(jnp.bfloat16), 'tensor')]
  transfers between devices with their start and end apart: 18 -> 10, of which waited for: 12 -> 8; matrix products, arithmetic and copies ran while one was open for 31% -> 6% of each run, Pallas kernels for 0% -> 12%
where the time goes in v1:
time: 451 us; the launch traced here: 445 us
  waiting for transfers between devices  180 us (40%)
  Pallas kernels  123 us (27%)
  blocking collectives  49 us (11%)
  starting transfers between devices  45.4 us (10%)
  local copies, waits for them, and re-layouts  18.4 us (4%)
  other arithmetic  18.2 us (4%)
  matrix products  10.4 us (2%)
    all_to_all x5, waiting for transfers between devices, exchange(): lax.all_to_all(values, 'expert', split_axis=0, concat_axis=0, tiled=True,...  168 us
    all_to_all x1, blocking collectives, exchange(): lax.all_to_all(values, 'expert', split_axis=0, concat_axis=0, tiled=True,...  49 us
    all_to_all x5, starting transfers between devices, exchange(): lax.all_to_all(values, 'expert', split_axis=0, concat_axis=0, tiled=True,...  44.5 us
    pallas_call x1, Pallas kernels, experts_call(): pl.pallas_call(expert_body, grid=(1,), in_specs=[whole(own.shape), whole(...  33.5 us
    pallas_call x1, Pallas kernels, attend_back(): pl.pallas_call(attend_back_body, grid=(pairs,), in_specs=[SMEM, col, col,...  28.1 us
    pallas_call x1, Pallas kernels, combine(): pl.pallas_call(combine_body, in_specs=[vmem] * 10, out_specs=[vmem] * 5,...  21.5 us
    pallas_call x1, Pallas kernels, attend(): pl.pallas_call(attend_body, grid=(PARTS, pairs), in_specs=[SMEM, pl.Block...  16 us
    ppermute x5, waiting for transfers between devices, swap(): return lax.ppermute(values, 'tensor', [(0, 1), (1, 0)])  12.5 us
  transfers between devices with their start and end apart: 10, of which 8 were waited for; matrix products, arithmetic and copies ran while one was open for 6% of the time, Pallas kernels for 12%

profile of v1, /device:TPU:0, one launch (start us, length us, event | category | flops | bytes accessed | tf_op | source)
XLA Modules:
  0.0 445.4 jit_solution(2286442880289991209)
XLA Ops:
  0.7 1.3 reshape.94.gain_ref
  1.9 0.9 convert_reduce_fusion.2
  2.8 0.7 bitcast_add_fusion
  3.5 3.7 negate_select_fusion
  7.2 1.2 pad_add_fusion.meta_ref
  8.5 6.6 %qkv.1 = (bf16[1024,768]{1,0:T(8,128)(2,1)}, bf16[1024,384]{1,0:T(8,128)(2,1)}, bf16[1024,384]{1,0:T(8,128)(2,1)}, bf16[1024,384]{1,0:T(8,128)(2,1)}) custom-call(bf16[1024,768]{1,0:T(8,128)(2,1)} %h_ref.5, f32[1,768]{1,0:T(1,128)} %reshape.94.gain_ref, bf16[3,768,384]{2,1,0:T(8,128)(2,1)} %bitcast.80, f32[1024,128]{1,0:T(8,128)} %get-tuple-element.67.cos_ref, ...), custom_call_target="tpu_custom_call" | custom-call | flops 1811939328 | bytes 10485760 | tf_op jit(solution)/shard_map/qkv/pallas_call | solution.py:81
  15.0 16.0 %attend.1 = (bf16[1024,384]{1,0:T(8,128)(2,1)}, f32[8,1024]{1,0:T(8,128)}) custom-call(s32[8]{0:T(128)} %pad_add_fusion.meta_ref, bf16[1024,384]{1,0:T(8,128)(2,1)} %get-tuple-element.37.q_ref, bf16[1024,384]{1,0:T(8,128)(2,1)} %get-tuple-element.38.k_ref, bf16[1024,384]{1,0:T(8,128)(2,1)} %get-tuple-element.39.v_ref), custom_call_target="tpu_custom_call" | custom-call | flops 1610612736 | bytes 8388608 | tf_op jit(solution)/shard_map/attend/pallas_call | solution.py:172
  31.1 2.1 fusion.2.a_ref
  33.2 0.5 collective-permute-start
  33.7 1.0 reshape.95.gain_ref
  34.7 0.6 pad_maximum_fusion.3.joint_ref
  35.3 3.8 collective-permute-done.b_ref
  39.1 11.6 %mid.1 = (f32[1024,768]{1,0:T(8,128)}, bf16[1024,768]{1,0:T(8,128)(2,1)}, bf16[704,1536]{1,0:T(8,128)(2,1)}, f32[16,1024]{1,0:T(8,128)}, f32[1024,128]{1,0:T(8,128)}) custom-call(s32[1]{0:T(128)} %bitcast.tid_ref, bf16[1024,768]{1,0:T(8,128)(2,1)} %h_ref.5, f32[1024,768]{1,0:T(8,128)} %copy-done, f32[1024,768]{1,0:T(8,128)} %collective-permute-done.b_ref, ...), custom_call_target="tpu_custom_call" | custom-call | flops 2214592512 | bytes 16777216 | tf_op jit(solution)/shard_map/mid/pallas_call | solution.py:421
  50.7 6.2 %all-to-all-start = ((bf16[8,88,1536]{2,1,0:T(8,128)(2,1)}), bf16[8,88,1536]{2,1,0:T(8,128)(2,1)}, u32[]{:S(2)}, u32[]{:S(2)}) async-start(bf16[8,88,1536]{2,1,0:T(8,128)(2,1)} %bitcast.79), calls=%async_computation | async-start | bytes 4325376 | tf_op jit(solution)/shard_map/all_to_all | solution.py:695
  56.9 1.6 pad_maximum_fusion
  58.6 25.3 %all-to-all-done = bf16[8,88,1536]{2,1,0:T(8,128)(2,1)} async-done(((bf16[8,88,1536]{2,1,0:T(8,128)(2,1)}), bf16[8,88,1536]{2,1,0:T(8,128)(2,1)}, u32[]{:S(2)}, u32[]{:S(2)}) %all-to-all-start) | async-done | bytes 2162720 | tf_op jit(solution)/shard_map/all_to_all | solution.py:695
  83.9 2.9 broadcast_in_dim.24
  86.7 8.2 %all-to-all-start.1 = ((bf16[16,144,1024]{2,1,0:T(8,128)(2,1)}), bf16[16,144,1024]{2,1,0:T(8,128)(2,1)}, u32[]{:S(2)}, u32[]{:S(2)}) async-start(bf16[16,144,1024]{2,1,0:T(8,128)(2,1)} %bitcast.73), calls=%async_computation.1 | async-start | bytes 9437184 | tf_op jit(solution)/shard_map/all_to_all | solution.py:695
  95.0 87.5 %all-to-all-done.1 = bf16[16,144,1024]{2,1,0:T(8,128)(2,1)} async-done(((bf16[16,144,1024]{2,1,0:T(8,128)(2,1)}), bf16[16,144,1024]{2,1,0:T(8,128)(2,1)}, u32[]{:S(2)}, u32[]{:S(2)}) %all-to-all-start.1) | async-done | bytes 4718624 | tf_op jit(solution)/shard_map/all_to_all | solution.py:695
  182.5 1.3 copy-done.16
  183.8 33.5 %experts.1 = (bf16[704,1536]{1,0:T(8,128)(2,1)}, bf16[704,1536]{1,0:T(8,128)(2,1)}, bf16[16,3,48,1024]{3,2,1,0:T(8,128)(2,1)}) custom-call(bf16[704,1536]{1,0:T(8,128)(2,1)} %bitcast.9.own_ref, bf16[704,1536]{1,0:T(8,128)(2,1)} %copy-done.16, bf16[16,3,48,1024]{3,2,1,0:T(8,128)(2,1)} %bitcast.15.wg_ref.wu_ref.wd_ref, ...), custom_call_target="tpu_custom_call" | custom-call | flops 19931332608 | bytes 23068672 | tf_op jit(solution)/shard_map/experts/pallas_call | solution.py:503
  217.3 4.5 %collective-permute-done.2 = bf16[704,1536]{1,0:T(8,128)(2,1)S(1)} collective-permute-done((bf16[704,1536]{1,0:T(8,128)(2,1)}, bf16[704,1536]{1,0:T(8,128)(2,1)S(1)}, u32[]{:S(2)}, u32[]{:S(2)}) %collective-permute-start.2) | collective-permute-done | bytes 2162720 | tf_op jit(solution)/shard_map/ppermute | solution.py:701
  221.8 2.2 add.21
  224.0 49.0 %all_to_all.30 = bf16[8,88,1536]{2,1,0:T(8,128)(2,1)S(1)} all-to-all(bf16[8,88,1536]{2,1,0:T(8,128)(2,1)S(1)} %bitcast.75), channel_id=1, replica_groups={{0,2,4,6,8,10,12,14},{16,18,20,22,24,26,28,30},{1,3,5,7,9,11,13,15},{17..., dimensions={0} | all-to-all | bytes 4325376 | tf_op jit(solution)/shard_map/all_to_all | solution.py:695
  272.9 4.8 %all-to-all-start.5 = ((bf16[16,144,1024]{2,1,0:T(8,128)(2,1)}), bf16[16,144,1024]{2,1,0:T(8,128)(2,1)}, u32[]{:S(2)}, u32[]{:S(2)}) async-start(bf16[16,144,1024]{2,1,0:T(8,128)(2,1)} %bitcast.76), calls=%async_computation.5 | async-start | bytes 9437184 | tf_op jit(solution)/shard_map/all_to_all | solution.py:695
  277.8 4.2 collective-permute-done.3.oth_ref
  282.1 1.3 copy-done.15
  283.4 21.5 %combine.1 = (bf16[1024,768]{1,0:T(8,128)(2,1)}, f32[12,1024]{1,0:T(8,128)}, f32[1024,768]{1,0:T(8,128)}, bf16[1024,768]{1,0:T(8,128)(2,1)}, f32[24,768]{1,0:T(8,128)}) custom-call(bf16[704,1536]{1,0:T(8,128)(2,1)} %bitcast.78, bf16[704,1536]{1,0:T(8,128)(2,1)} %copy-done.15, f32[1024,768]{1,0:T(8,128)} %get-tuple-element.44.r_ref, ...), custom_call_target="tpu_custom_call" | custom-call | flops 6643777536 | bytes 23068672 | tf_op jit(solution)/shard_map/combine/pallas_call | solution.py:637
  304.9 28.1 %attend_back.1 = (bf16[1024,384]{1,0:T(8,128)(2,1)}, bf16[1024,384]{1,0:T(8,128)(2,1)}, bf16[1024,384]{1,0:T(8,128)(2,1)}) custom-call(s32[8]{0:T(128)} %pad_add_fusion.meta_ref, bf16[1024,384]{1,0:T(8,128)(2,1)} %get-tuple-element.37.q_ref, bf16[1024,384]{1,0:T(8,128)(2,1)} %get-tuple-element.38.k_ref, bf16[1024,384]{1,0:T(8,128)(2,1)} %get-tuple-element.39.v_ref, ...), custom_call_target="tpu_custom_call" | custom-call | flops 4026531840 | bytes 12582912 | tf_op jit(solution)/shard_map/attend_back/pallas_call | solution.py:281
  333.0 2.2 fusion
  335.3 1.0 fusion.1
  336.3 0.1 copy-done.6
  336.4 1.0 add_convert_fusion.a_ref
  337.4 0.2 collective-permute-start.4
  337.6 0.2 copy-done.17
  337.9 1.0 convolution_convert_fusion.3
  338.9 0.2 copy-done.8
  339.1 1.0 convolution_convert_fusion.2
  340.1 1.0 convolution_convert_fusion.1
  341.3 0.5 copy-done.18
  341.8 1.0 convolution_convert_fusion
  342.8 1.1 copy-done.4
  344.0 5.7 %final.1 = (bf16[1024,768]{1,0:T(8,128)(2,1)}, f32[8,768]{1,0:T(8,128)}) custom-call(bf16[1024,768]{1,0:T(8,128)(2,1)} %h_ref.5, f32[1,768]{1,0:T(1,128)} %reshape.94.gain_ref, f32[1024,768]{1,0:T(8,128)} %get-tuple-element.49.rg_ref, bf16[1024,768]{1,0:T(8,128)(2,1)} %copy-done.1, bf16[1024,768]{1,0:T(8,128)(2,1)} %copy-done.4), custom_call_target="tpu_custom_call" | custom-call | flops 15728640 | bytes 9437184 | tf_op jit(solution)/shard_map/final/pallas_call | solution.py:679
  349.7 0.7 slice.59
  350.4 0.1 reshape.106
  350.6 0.8 reshape.109
  351.4 13.5 %all-to-all-done.5 = bf16[16,144,1024]{2,1,0:T(8,128)(2,1)} async-done(((bf16[16,144,1024]{2,1,0:T(8,128)(2,1)}), bf16[16,144,1024]{2,1,0:T(8,128)(2,1)}, u32[]{:S(2)}, u32[]{:S(2)}) %all-to-all-start.5) | async-done | bytes 4718624 | tf_op jit(solution)/shard_map/all_to_all | solution.py:695
  364.9 21.6 %all-to-all-start.4 = ((f32[16,1,1152]{2,1,0:T(1,128)}), f32[16,1,1152]{2,1,0:T(1,128)S(1)}, u32[]{:S(2)}, u32[]{:S(2)}) async-start(f32[16,1,1152]{2,1,0:T(1,128)} %reshape.109), calls=%async_computation.4 | async-start | bytes 147456 | tf_op jit(solution)/shard_map/all_to_all | solution.py:695
  386.5 1.8 pad_maximum_fusion.1
  388.3 5.8 %all-to-all-done.4 = f32[16,1,1152]{2,1,0:T(1,128)S(1)} async-done(((f32[16,1,1152]{2,1,0:T(1,128)}), f32[16,1,1152]{2,1,0:T(1,128)S(1)}, u32[]{:S(2)}, u32[]{:S(2)}) %all-to-all-start.4) | async-done | bytes 73760 | tf_op jit(solution)/shard_map/all_to_all | solution.py:695
  394.0 3.7 all-to-all-start.3
  397.8 4.2 convert_reduce_fusion
  402.0 2.3 slice_bitcast_fusion
  404.3 0.5 broadcast.12
  404.8 0.8 reduce.1
  405.6 0.1 reshape.110
  405.8 0.6 slice.78
  406.3 0.5 slice_bitcast_fusion.12
  406.9 0.6 slice_bitcast_fusion.11
  407.4 0.6 slice_bitcast_fusion.10
  408.0 35.7 %all-to-all-done.3 = bf16[16,192,384]{2,1,0:T(8,128)(2,1)S(1)} async-done(((bf16[16,192,384]{2,1,0:T(8,128)(2,1)}), bf16[16,192,384]{2,1,0:T(8,128)(2,1)S(1)}, u32[]{:S(2)}, u32[]{:S(2)}) %all-to-all-start.3) | async-done | bytes 2359328 | tf_op jit(solution)/shard_map/all_to_all | solution.py:695
  443.7 0.3 convert_reduce_fusion.1
  444.0 0.7 slice.72
  444.7 0.6 slice_bitcast_fusion.9
  (42 shorter events, 0.4 us)
Async XLA Ops:
  15.0 16.0 %copy-start.10 = (bf16[384,768]{1,0:T(8,128)(2,1)S(1)}, bf16[384,768]{1,0:T(8,128)(2,1)}, u32[]{:S(2)}) copy-start(bf16[384,768]{1,0:T(8,128)(2,1)} %wo_ref.1) | copy-start | bytes 1769476
  31.0 2.7 copy-start.14
  31.0 3.7 copy-start.12
  31.0 3.7 copy-start.13
  33.2 6.0 %copy-start = (f32[1024,768]{1,0:T(8,128)}, f32[1024,768]{1,0:T(8,128)S(1)}, u32[]{:S(2)}) copy-start(f32[1024,768]{1,0:T(8,128)S(1)} %fusion.2.a_ref) | copy-start | bytes 9437188
  33.2 6.0 %collective-permute-start = (f32[1024,768]{1,0:T(8,128)S(1)}, f32[1024,768]{1,0:T(8,128)}, u32[]{:S(2)}, u32[]{:S(2)}) collective-permute-start(f32[1024,768]{1,0:T(8,128)S(1)} %fusion.2.a_ref), channel_id=1, source_target_pairs={{0,1},{1,0},{2,3},{3,2},{4,5},{5,4},{6,7},{7,6},{8,9},{9,8},{10,11... | collective-permute-start | bytes 9437192 | tf_op jit(solution)/shard_map/ppermute | solution.py:701
  50.7 6.2 %copy-start.5 = (bf16[8,48,1024]{2,1,0:T(8,128)(2,1)S(1)}, bf16[8,48,1024]{2,1,0:T(8,128)(2,1)}, u32[]{:S(2)}) copy-start(bf16[8,48,1024]{2,1,0:T(8,128)(2,1)} %param.29) | copy-start | bytes 2359300
  50.7 33.1 %all-to-all-start = ((bf16[8,88,1536]{2,1,0:T(8,128)(2,1)}), bf16[8,88,1536]{2,1,0:T(8,128)(2,1)}, u32[]{:S(2)}, u32[]{:S(2)}) async-start(bf16[8,88,1536]{2,1,0:T(8,128)(2,1)} %bitcast.79), calls=%async_computation | async-start | bytes 4325376 | tf_op jit(solution)/shard_map/all_to_all | solution.py:695
  86.7 95.8 %all-to-all-start.1 = ((bf16[16,144,1024]{2,1,0:T(8,128)(2,1)}), bf16[16,144,1024]{2,1,0:T(8,128)(2,1)}, u32[]{:S(2)}, u32[]{:S(2)}) async-start(bf16[16,144,1024]{2,1,0:T(8,128)(2,1)} %bitcast.73), calls=%async_computation.1 | async-start | bytes 9437184 | tf_op jit(solution)/shard_map/all_to_all | solution.py:695
  95.0 87.6 %collective-permute-start.1 = (bf16[704,1536]{1,0:T(8,128)(2,1)}, bf16[704,1536]{1,0:T(8,128)(2,1)S(1)}, u32[]{:S(2)}, u32[]{:S(2)}) collective-permute-start(bf16[704,1536]{1,0:T(8,128)(2,1)} %bitcast.9.own_ref), channel_id=1, source_target_pairs={{0,1},{1,0},{2,3},{3,2},{4,5},{5,4},{6,7},{7,6},{8,9},{9,8},{10,11... | collective-permute-start | bytes 6488072 | tf_op jit(solution)/shard_map/ppermute | solution.py:701
  182.5 1.3 copy-start.16
  217.3 4.5 %collective-permute-start.2 = (bf16[704,1536]{1,0:T(8,128)(2,1)}, bf16[704,1536]{1,0:T(8,128)(2,1)S(1)}, u32[]{:S(2)}, u32[]{:S(2)}) collective-permute-start(bf16[704,1536]{1,0:T(8,128)(2,1)} %get-tuple-element.43), channel_id=1, source_target_pairs={{0,1},{1,0},{2,3},{3,2},{4,5},{5,4},{6,7},{7,6},{8,9},{9,8},{10,11... | collective-permute-start | bytes 6488072 | tf_op jit(solution)/shard_map/ppermute | solution.py:701
  272.9 4.8 %copy-start.2 = (bf16[8,88,1536]{2,1,0:T(8,128)(2,1)}, bf16[8,88,1536]{2,1,0:T(8,128)(2,1)S(1)}, u32[]{:S(2)}) copy-start(bf16[8,88,1536]{2,1,0:T(8,128)(2,1)S(1)} %all_to_all.30) | copy-start | bytes 6488068
  272.9 92.0 %all-to-all-start.5 = ((bf16[16,144,1024]{2,1,0:T(8,128)(2,1)}), bf16[16,144,1024]{2,1,0:T(8,128)(2,1)}, u32[]{:S(2)}, u32[]{:S(2)}) async-start(bf16[16,144,1024]{2,1,0:T(8,128)(2,1)} %bitcast.76), calls=%async_computation.5 | async-start | bytes 9437184 | tf_op jit(solution)/shard_map/all_to_all | solution.py:695
  277.7 4.3 collective-permute-start.3
  282.1 1.3 copy-start.15
  304.9 28.1 %copy-start.3 = (bf16[768,3,384]{2,0,1:T(8,128)(2,1)S(1)}, bf16[768,3,384]{2,0,1:T(8,128)(2,1)}, u32[]{:S(2)}) copy-start(bf16[768,3,384]{2,0,1:T(8,128)(2,1)} %param.20) | copy-start | bytes 5308420
  333.0 2.2 copy-start.9
  335.3 1.1 copy-start.6
  336.4 1.2 copy-start.11
  336.4 1.4 copy-start.17
  337.4 1.5 copy-start.1
  337.4 5.4 %collective-permute-start.4 = (bf16[1024,768]{1,0:T(8,128)(2,1)S(1)}, bf16[1024,768]{1,0:T(8,128)(2,1)S(1)}, u32[]{:S(2)}, u32[]{:S(2)}) collective-permute-start(bf16[1024,768]{1,0:T(8,128)(2,1)S(1)} %add_convert_fusion.a_ref), channel_id=1, source_target_pairs={{0,1},{1,0},{2,3},{3,2},{4,5},{5,4},{6,7},{7,6},{8,9},{9,8},{10,11... | collective-permute-start | bytes 4718600 | tf_op jit(solution)/shard_map/ppermute | solution.py:701
  337.9 1.3 copy-start.8
  340.1 1.1 copy-start.7
  340.1 1.6 copy-start.18
  342.8 1.1 copy-start.4
  364.9 29.1 %all-to-all-start.4 = ((f32[16,1,1152]{2,1,0:T(1,128)}), f32[16,1,1152]{2,1,0:T(1,128)S(1)}, u32[]{:S(2)}, u32[]{:S(2)}) async-start(f32[16,1,1152]{2,1,0:T(1,128)} %reshape.109), calls=%async_computation.4 | async-start | bytes 147456 | tf_op jit(solution)/shard_map/all_to_all | solution.py:695
  394.0 49.7 %all-to-all-start.3 = ((bf16[16,192,384]{2,1,0:T(8,128)(2,1)}), bf16[16,192,384]{2,1,0:T(8,128)(2,1)S(1)}, u32[]{:S(2)}, u32[]{:S(2)}) async-start(bf16[16,192,384]{2,1,0:T(8,128)(2,1)} %pad_maximum_fusion.1), calls=%async_computation.3 | async-start | bytes 4718592 | tf_op jit(solution)/shard_map/all_to_all | solution.py:695
